TPU v7x, 128 devices: a whole 4x4x4 slice. The times are simulated.
128 devices in a mesh: cams: 128 (over x, y, z, core).
Axes of the slice: x: 4, y: 4, z: 4, core: 2. Of those that a mesh axis runs over, the one named last changes fastest.
Arguments:
- right_side: float32 [512, 288], P('cams')
- schur_tiles: float32 [512, 4, 288, 288], P('cams')
- block_cols: int32 [512, 4], P('cams'), may hold values from 0 to 511, as said below
- tile_counts: int32 [512], P('cams'), may hold values from 1 to 4, as said below
- jacobi_inverse: float32 [512, 288, 288], P('cams'), as said below
Outputs:
- camera_update: float32 [512, 288], P('cams')
- final_residual: float32 [512, 288], P('cams')
Inputs may be any that keep to these rules, and one draw needn't show every extreme that they name: block_cols[g, 0] = g; the other slots of row g hold distinct blocks (g + o) mod 512 with 1 <= o <= 8. `tile_counts`: slot 0 is always live; some block row has all 4 slots live. `jacobi_inverse`: every tile is symmetric positive definite.
All inputs are finite; a program needn't handle non-finite values.
Results may differ from a plain program's by a relative error of at most 0.00025.
Values sent between devices are 32-bit elements; how exact they have to be, the bound alone decides.
A program may use at most 64 MiB of HBM per device.

v0:
```python
import jax
import jax.numpy as jnp
from jax import lax
from jax.sharding import PartitionSpec as P

BAND = 2
ITERS = 2


HIGH = lax.Precision.HIGHEST


def shifted(value, axis, steps):
    count = lax.axis_size(axis)
    pairs = [(source, (source + steps) % count) for source in range(count)]
    return lax.ppermute(value, axis, pairs)


def apply_schur(schur_tiles, block_cols, tile_counts, vector):
    blocks, slots = block_cols.shape
    slot_ids = lax.broadcasted_iota(jnp.int32, (blocks, slots), 1)
    live = slot_ids < tile_counts[:, None]
    transposed = live & (slot_ids > 0)
    offset = lax.axis_index("cams") * blocks
    total = blocks * lax.axis_size("cams")
    pieces = [vector]
    for distance in range(1, BAND + 1):
        pieces.append(shifted(vector, "cams", -distance))
    extended = jnp.concatenate(pieces, axis=0)
    local = (block_cols - offset) % total
    picked = extended[local]
    upper = jnp.einsum("bsij,bsj->bsi", schur_tiles, picked, precision=HIGH)
    result = jnp.sum(jnp.where(live[:, :, None], upper, 0.0), axis=1)
    lower = jnp.einsum("bsij,bi->bsj", schur_tiles, vector, precision=HIGH)
    lower = jnp.where(transposed[:, :, None], lower, 0.0)
    targets = extended.shape[0]
    onehot = (
        local.reshape(-1)[:, None] == lax.broadcasted_iota(jnp.int32, (1, targets), 1)
    ).astype(jnp.float32)
    spread = jnp.einsum("rt,rj->tj", onehot, lower.reshape(blocks * slots, -1), precision=HIGH)
    result = result + spread[:blocks]
    for distance in range(1, BAND + 1):
        result = result + shifted(
            spread[distance * blocks : (distance + 1) * blocks], "cams", distance
        )
    return result


def apply_precond(jacobi_inverse, vector):
    return jnp.einsum("bij,bj->bi", jacobi_inverse, vector, precision=HIGH)


def inner_norm(residual, precond):
    return lax.psum(jnp.sum(residual * precond), "cams")


def on_device(right_side, schur_tiles, block_cols, tile_counts, jacobi_inverse):
    camera_update = jnp.zeros_like(right_side)
    final_residual = right_side
    precond = apply_precond(jacobi_inverse, final_residual)
    norm_now = inner_norm(final_residual, precond)
    direction = precond
    for iteration in range(ITERS):
        image = apply_schur(schur_tiles, block_cols, tile_counts, direction)
        alpha = norm_now / lax.psum(jnp.sum(direction * image), "cams")
        camera_update = camera_update + alpha * direction
        final_residual = final_residual - alpha * image
        if iteration + 1 < ITERS:
            precond = apply_precond(jacobi_inverse, final_residual)
            fresh = inner_norm(final_residual, precond)
            direction = precond + fresh / norm_now * direction
            norm_now = fresh
    return (camera_update, final_residual)


def solution(mesh):
    placed = (
        P("cams", None),
        P("cams", None, None, None),
        P("cams", None),
        P("cams"),
        P("cams", None, None),
    )
    return jax.shard_map(
        on_device,
        mesh=mesh,
        in_specs=placed,
        out_specs=(P("cams", None), P("cams", None)),
        check_vma=False,
    )
```

profile of v0, /device:TPU:1, one launch (start us, length us, event | category | flops | bytes accessed | tf_op | source)
XLA Modules:
  0.0 255.7 jit_solution(14860894839681979014)
XLA Ops:
  0.6 0.0 copy-start
  0.6 1.5 copy-done
  2.1 2.3 fusion.15
  4.5 1.4 collective-permute-start
  5.9 8.5 %collective-permute-start.1 = (f32[4,288]{1,0:T(4,128)S(1)}, f32[4,288]{1,0:T(4,128)S(1)}, u32[]{:S(2)}, u32[]{:S(2)}) collective-permute-start(f32[4,288]{1,0:T(4,128)S(1)} %bitcast.47), channel_id=1, source_target_pairs={{0,126},{1,127},{2,0},{3,1},{4,2},{5,3},{6,4},{7,5},{8,6},{9,7},{1... | collective-permute-start | bytes 13832 | tf_op jit(solution)/shard_map/ppermute | solution.py:16
  14.4 0.7 compare_select_fusion
  15.1 0.1 eq.11
  15.2 0.7 iota_compare_fusion.3
  15.9 0.0 copy-start.1
  15.9 5.7 %fusion.13 = f32[4,1,4,288]{3,1,2,0:T(1,128)S(1)} fusion(f32[4,4,288,288]{3,2,1,0:T(8,128)} %param.6, f32[4,288,1,1]{1,0,2,3:T(4,128)S(1)} %bitcast.48), kind=kOutput, calls=%fused_computation.26 | convolution fusion | flops 15925248 | bytes 5331456 | tf_op jit(solution)/shard_map/bsij,bi->bsj/dot_general | solution.py:34
  21.6 0.1 bitcast_select_fusion.2
  21.7 0.3 fusion.3
  22.0 1.4 collective-permute-start.2
  23.4 0.0 collective-permute-start.3
  23.4 0.1 reshape.63
  23.5 0.0 collective-permute-done
  23.5 0.0 collective-permute-done.1
  23.6 0.6 gather_fusion
  24.2 8.2 %fusion.24 = f32[4,4,1,288]{3,2,1,0:T(1,128)S(1)} fusion(f32[4,4,288,1]{2,3,1,0:T(1,128)S(1)} %reshape.94, f32[4,4,288,288]{3,2,1,0:T(8,128)} %param.6), kind=kOutput, calls=%fused_computation.51 | convolution fusion | flops 15925248 | bytes 5345280 | tf_op jit(solution)/shard_map/bsij,bsj->bsi/dot_general | solution.py:32
  32.4 0.1 fusion.1
  32.5 0.0 collective-permute-done.2
  32.5 0.0 collective-permute-done.3
  32.5 0.0 copy-done.1
  32.5 0.6 multiply_reduce_fusion.1
  33.1 66.4 %all-reduce = (f32[]{:T(128)}, f32[]{:T(128)}) all-reduce(f32[]{:T(128)} %get-tuple-element.3, f32[]{:T(128)} %get-tuple-element.2), channel_id=1, replica_groups=mesh['cams'=128] {'cams'}, use_global_device_ids=true, to_apply=%region_1.0 | all-reduce | flops 2 | bytes 16 | tf_op jit(solution)/shard_map/psum | solution.py:54
  100.9 1.6 fusion.11
  102.5 0.6 fusion.8
  103.1 62.6 %psum.30 = f32[]{:T(128)} all-reduce(f32[]{:T(128)} %fusion.8), channel_id=1, replica_groups=mesh['cams'=128] {'cams'}, use_global_device_ids=true, to_apply=%region_6.7 | all-reduce | flops 1 | bytes 8 | tf_op jit(solution)/shard_map/psum | solution.py:54
  167.0 2.9 %collective-permute-start.5 = (f32[4,288]{1,0:T(4,128)S(1)}, f32[4,288]{1,0:T(4,128)S(1)}, u32[]{:S(2)}, u32[]{:S(2)}) collective-permute-start(f32[4,288]{1,0:T(4,128)S(1)} %bitcast_add_fusion), channel_id=1, source_target_pairs={{0,126},{1,127},{2,0},{3,1},{4,2},{5,3},{6,4},{7,5},{8,6},{9,7},{1... | collective-permute-start | bytes 13832 | tf_op jit(solution)/shard_map/ppermute | solution.py:16
  170.0 1.0 collective-permute-start.4
  170.9 5.7 %fusion.9 = f32[4,1,4,288]{3,1,2,0:T(1,128)S(1)} fusion(f32[4,4,288,288]{3,2,1,0:T(8,128)} %param.6, f32[4,288,1,1]{1,0,2,3:T(4,128)S(1)} %bitcast.44), kind=kOutput, calls=%fused_computation.22 | convolution fusion | flops 15925248 | bytes 5331456 | tf_op jit(solution)/shard_map/bsij,bi->bsj/dot_general | solution.py:34
  176.6 0.1 bitcast_select_fusion
  176.7 0.3 fusion.2
  177.0 0.9 collective-permute-start.6
  177.9 0.0 collective-permute-start.7
  177.9 0.0 collective-permute-done.5
  177.9 0.0 collective-permute-done.4
  177.9 0.6 gather_fusion.1
  178.5 8.2 %fusion.25 = f32[4,4,1,288]{3,2,1,0:T(1,128)S(1)} fusion(f32[4,4,288,1]{2,3,1,0:T(1,128)S(1)} %reshape.96, f32[4,4,288,288]{3,2,1,0:T(8,128)} %param.6), kind=kOutput, calls=%fused_computation.52 | convolution fusion | flops 15925248 | bytes 5345280 | tf_op jit(solution)/shard_map/bsij,bsj->bsi/dot_general | solution.py:32
  186.7 0.1 fusion
  186.8 0.0 collective-permute-done.6
  186.8 0.0 collective-permute-done.7
  186.8 0.6 multiply_reduce_fusion
  187.4 66.3 %psum.31 = f32[]{:T(128)} all-reduce(f32[]{:T(128)} %get-tuple-element.6), channel_id=1, replica_groups=mesh['cams'=128] {'cams'}, use_global_device_ids=true, to_apply=%region_9.10 | all-reduce | flops 1 | bytes 8 | tf_op jit(solution)/shard_map/psum | solution.py:65
  255.1 0.6 multiply_subtract_fusion
  (13 shorter events, 0.2 us)
Async XLA Ops:
  0.6 1.5 copy-start
  4.5 19.1 %collective-permute-start = (f32[4,288]{1,0:T(4,128)S(1)}, f32[4,288]{1,0:T(4,128)S(1)}, u32[]{:S(2)}, u32[]{:S(2)}) collective-permute-start(f32[4,288]{1,0:T(4,128)S(1)} %bitcast.46), channel_id=1, source_target_pairs={{0,127},{1,0},{2,1},{3,2},{4,3},{5,4},{6,5},{7,6},{8,7},{9,8},{10,... | collective-permute-start | bytes 13832 | tf_op jit(solution)/shard_map/ppermute | solution.py:16
  5.9 17.6 %collective-permute-start.1 = (f32[4,288]{1,0:T(4,128)S(1)}, f32[4,288]{1,0:T(4,128)S(1)}, u32[]{:S(2)}, u32[]{:S(2)}) collective-permute-start(f32[4,288]{1,0:T(4,128)S(1)} %bitcast.47), channel_id=1, source_target_pairs={{0,126},{1,127},{2,0},{3,1},{4,2},{5,3},{6,4},{7,5},{8,6},{9,7},{1... | collective-permute-start | bytes 13832 | tf_op jit(solution)/shard_map/ppermute | solution.py:16
  15.9 16.6 %copy-start.1 = (f32[4,288]{1,0:T(4,128)S(1)}, f32[4,288]{1,0:T(4,128)}, u32[]{:S(2)}) copy-start(f32[4,288]{1,0:T(4,128)} %param.5) | copy-start | bytes 13828
  22.0 10.5 %collective-permute-start.2 = (f32[4,288]{1,0:T(4,128)S(1)}, f32[4,288]{1,0:T(4,128)S(1)}, u32[]{:S(2)}, u32[]{:S(2)}) collective-permute-start(f32[4,288]{1,0:T(4,128)S(1)} %get-tuple-element.13), channel_id=1, source_target_pairs={{0,1},{1,2},{2,3},{3,4},{4,5},{5,6},{6,7},{7,8},{8,9},{9,10},{10,1... | collective-permute-start | bytes 13832 | tf_op jit(solution)/shard_map/ppermute | solution.py:16
  23.4 9.1 %collective-permute-start.3 = (f32[4,288]{1,0:T(4,128)S(1)}, f32[4,288]{1,0:T(4,128)S(1)}, u32[]{:S(2)}, u32[]{:S(2)}) collective-permute-start(f32[4,288]{1,0:T(4,128)S(1)} %get-tuple-element.14), channel_id=1, source_target_pairs={{0,2},{1,3},{2,4},{3,5},{4,6},{5,7},{6,8},{7,9},{8,10},{9,11},{10,... | collective-permute-start | bytes 13832 | tf_op jit(solution)/shard_map/ppermute | solution.py:16
  167.0 10.8 %collective-permute-start.5 = (f32[4,288]{1,0:T(4,128)S(1)}, f32[4,288]{1,0:T(4,128)S(1)}, u32[]{:S(2)}, u32[]{:S(2)}) collective-permute-start(f32[4,288]{1,0:T(4,128)S(1)} %bitcast_add_fusion), channel_id=1, source_target_pairs={{0,126},{1,127},{2,0},{3,1},{4,2},{5,3},{6,4},{7,5},{8,6},{9,7},{1... | collective-permute-start | bytes 13832 | tf_op jit(solution)/shard_map/ppermute | solution.py:16
  170.0 7.9 %collective-permute-start.4 = (f32[4,288]{1,0:T(4,128)S(1)}, f32[4,288]{1,0:T(4,128)S(1)}, u32[]{:S(2)}, u32[]{:S(2)}) collective-permute-start(f32[4,288]{1,0:T(4,128)S(1)} %bitcast_add_fusion), channel_id=1, source_target_pairs={{0,127},{1,0},{2,1},{3,2},{4,3},{5,4},{6,5},{7,6},{8,7},{9,8},{10,... | collective-permute-start | bytes 13832 | tf_op jit(solution)/shard_map/ppermute | solution.py:16
  177.0 9.8 %collective-permute-start.6 = (f32[4,288]{1,0:T(4,128)S(1)}, f32[4,288]{1,0:T(4,128)S(1)}, u32[]{:S(2)}, u32[]{:S(2)}) collective-permute-start(f32[4,288]{1,0:T(4,128)S(1)} %get-tuple-element.11), channel_id=1, source_target_pairs={{0,1},{1,2},{2,3},{3,4},{4,5},{5,6},{6,7},{7,8},{8,9},{9,10},{10,1... | collective-permute-start | bytes 13832 | tf_op jit(solution)/shard_map/ppermute | solution.py:16
  177.9 9.0 %collective-permute-start.7 = (f32[4,288]{1,0:T(4,128)S(1)}, f32[4,288]{1,0:T(4,128)S(1)}, u32[]{:S(2)}, u32[]{:S(2)}) collective-permute-start(f32[4,288]{1,0:T(4,128)S(1)} %get-tuple-element.12), channel_id=1, source_target_pairs={{0,2},{1,3},{2,4},{3,5},{4,6},{5,7},{6,8},{7,9},{8,10},{9,11},{10,... | collective-permute-start | bytes 13832 | tf_op jit(solution)/shard_map/ppermute | solution.py:16
where the time goes:
time: 256 us
  blocking collectives  195 us (76%)
  matrix products  32.3 us (13%)
  starting transfers between devices  16.1 us (6%)
  between operations  4.8 us (2%)
  other arithmetic  4.27 us (2%)
  local copies, waits for them, and re-layouts  2.91 us (1%)
    psum x2, blocking collectives, inner_norm(): return lax.psum(jnp.sum(residual * precond), 'cams')  129 us
    psum x1, blocking collectives, on_device(): alpha = norm_now / lax.psum(jnp.sum(direction * image), 'cams')  66.3 us
    dot_general x2, matrix products, apply_schur(): upper = jnp.einsum('bsij,bsj->bsi', schur_tiles, picked, precision=HIGH)  16.4 us
    ppermute x8, starting transfers between devices, shifted(): return lax.ppermute(value, axis, pairs)  16.1 us
    dot_general x2, matrix products, apply_schur(): lower = jnp.einsum('bsij,bi->bsj', schur_tiles, vector, precision=HIGH)  11.4 us
  transfers between devices with their start and end apart: 8, of which 0 were waited for; matrix products, arithmetic and copies ran while one was open for 12% of the time, Pallas kernels for 0%

commit v1 on v0

v1 whole, which is shorter than its diff:
```python
import functools

import jax
import jax.numpy as jnp
from jax import lax
from jax.experimental import pallas as pl
from jax.experimental.pallas import tpu as pltpu
from jax.sharding import PartitionSpec as P

MESH = pl.DeviceIdType.MESH
LANES = 128
ROWS = 32
NEAR = 8
BAND = 2
AXIS = "cams"


def lane_groups(width):
    return [(start, min(start + LANES, width)) for start in range(0, width, LANES)]


def fold_rows(value):
    rows, width = value.shape
    return jnp.sum(value.reshape(rows // 8, 8, width), axis=0)


def kernel(
    n,
    rhs_hbm,
    tiles_hbm,
    cols_hbm,
    counts_hbm,
    minv_hbm,
    x_out,
    r_out,
    tiles,
    minv,
    rhs,
    cols,
    counts,
    p_col,
    q_col,
    p_ext,
    q_ext,
    s_row,
    w_row,
    prods,
    p_low,
    q_low,
    p_got,
    q_got,
    near_buf,
    far_buf,
    tile_sem,
    minv_sem,
    small_sem,
    halo_send,
    halo_recv,
    near_send,
    near_recv,
    far_send,
    far_recv,
):
    blocks, slots, width, _ = tiles.shape
    far = n // NEAR
    me = lax.axis_index(AXIS)
    mine = lax.rem(me, NEAR)
    plane = lax.div(me, NEAR)
    groups = lane_groups(width)
    chunks = width // ROWS

    small = [
        pltpu.make_async_copy(rhs_hbm, rhs, small_sem.at[0]),
        pltpu.make_async_copy(cols_hbm, cols, small_sem.at[1]),
        pltpu.make_async_copy(counts_hbm, counts, small_sem.at[2]),
    ]
    minv_copy = [
        pltpu.make_async_copy(minv_hbm.at[g], minv.at[g], minv_sem.at[g]) for g in range(blocks)
    ]
    tile_copy = {
        (g, k): pltpu.make_async_copy(
            tiles_hbm.at[g, k], tiles.at[g, k], tile_sem.at[g * slots + k]
        )
        for g in range(blocks)
        for k in range(slots)
    }
    small[0].start()
    for copy in minv_copy:
        copy.start()
    small[1].start()
    small[2].start()
    for k in list(range(1, slots)) + [0]:
        for g in range(blocks):
            tile_copy[g, k].start()

    def ahead(steps):
        return (lax.rem(me + n + steps, n),)

    def near_peer(steps):
        return (plane * NEAR + lax.rem(mine + NEAR + steps, NEAR),)

    def far_peer(steps):
        return (lax.rem(plane + far + steps, far) * NEAR + mine,)

    barrier = pltpu.get_barrier_semaphore()
    peers = [ahead(s) for s in (1, -1, 2, -2)]
    peers += [near_peer(s) for s in range(1, NEAR)]
    peers += [far_peer(s) for s in range(1, far)]
    for peer in peers:
        pl.semaphore_signal(barrier, inc=1, device_id=peer, device_id_type=MESH)

    def send(index, source, target, steps):
        return pltpu.make_async_remote_copy(
            src_ref=source,
            dst_ref=target,
            send_sem=halo_send.at[index],
            recv_sem=halo_recv.at[index],
            device_id=ahead(steps),
            device_id_type=MESH,
        )

    def eye(chunk):
        offset = (chunk * ROWS) % LANES
        lane = lax.broadcasted_iota(jnp.int32, (ROWS, LANES), 1)
        row = lax.broadcasted_iota(jnp.int32, (ROWS, LANES), 0)
        return lane == row + offset

    eyes = [eye(c) for c in range(LANES // ROWS)]

    def times_rows(terms, column, row_out):
        sums = [jnp.zeros((8, LANES), jnp.float32) for _ in groups]
        for c in range(chunks):
            rows = slice(c * ROWS, (c + 1) * ROWS)
            total = None
            for matrix, vector in terms:
                part = matrix[rows, :] * vector
                total = part if total is None else total + part
            value = jnp.sum(total, axis=1, keepdims=True)
            wide = jnp.broadcast_to(value, (ROWS, LANES))
            if column is not None:
                column[rows, :] = wide
            at = c * ROWS // LANES
            sums[at] = sums[at] + fold_rows(jnp.where(eyes[c % len(eyes)], wide, 0.0))
        for (low, high), value in zip(groups, sums):
            row_out[:, low:high] = jnp.sum(value, axis=0, keepdims=True)[:, : high - low]

    def times_columns(matrices, column, row_outs):
        sums = [[None for _ in groups] for _ in matrices]
        for c in range(chunks):
            rows = slice(c * ROWS, (c + 1) * ROWS)
            wide = column[rows, :]
            for index, matrix in enumerate(matrices):
                for at, (low, high) in enumerate(groups):
                    part = fold_rows(matrix[rows, low:high] * wide[:, : high - low])
                    before = sums[index][at]
                    sums[index][at] = part if before is None else before + part
        for index, row_out in enumerate(row_outs):
            for (low, high), value in zip(groups, sums[index]):
                row_out[:, low:high] = jnp.sum(value, axis=0, keepdims=True)

    small[0].wait()
    for g in range(blocks):
        minv_copy[g].wait()
        times_rows(
            [(minv.at[g], rhs[g : g + 1, :])], p_col.at[g], p_ext.at[0, g : g + 1, :]
        )

    pl.semaphore_wait(barrier, len(peers))
    p_sends = [send(d - 1, p_ext.at[0], p_ext.at[d], -d) for d in range(1, BAND + 1)]
    for copy in p_sends:
        copy.start()

    small[1].wait()
    small[2].wait()
    total_blocks = n * blocks
    places = {}
    lives = {}
    for g in range(blocks):
        for k in range(1, slots):
            local = lax.rem(cols[g, k] - me * blocks + total_blocks, total_blocks)
            live = k < counts[g]
            places[g, k] = jnp.where(live, local, 0)
            lives[g, k] = live

    row_ids = lax.broadcasted_iota(jnp.int32, (blocks, width), 0)

    def spread(distance):
        total = jnp.zeros((blocks, width), jnp.float32)
        for (g, k), place in places.items():
            slot = g * slots + k
            hit = row_ids == jnp.where(lives[g, k], place - distance * blocks, -1)
            total = total + jnp.where(hit, prods[slot : slot + 1, :], 0.0)
        return total

    def picked(ext, g, k):
        place = places[g, k]
        row = ext[lax.div(place, blocks), pl.ds(lax.rem(place, blocks), 1), :]
        return jnp.where(lives[g, k], row, 0.0)

    def slot_row(g, k):
        slot = g * slots + k
        return prods.at[slot : slot + 1, :]

    for g in range(blocks):
        for k in range(1, slots):
            tile_copy[g, k].wait()
        times_columns(
            [tiles.at[g, k] for k in range(1, slots)],
            p_col.at[g],
            [slot_row(g, k) for k in range(1, slots)],
        )
    for d in range(1, BAND + 1):
        p_low[d] = spread(d)
    low_sends = [send(BAND + d - 1, p_low.at[d], p_got.at[d], d) for d in range(1, BAND + 1)]
    for copy in low_sends:
        copy.start()
    p_low[0] = spread(0)

    for g in range(blocks):
        tile_copy[g, 0].wait()
    for copy in p_sends:
        copy.wait_recv()
    for g in range(blocks):
        terms = [(tiles.at[g, 0], p_ext[0, g : g + 1, :])]
        terms += [(tiles.at[g, k], picked(p_ext, g, k)) for k in range(1, slots)]
        times_rows(terms, None, s_row.at[g : g + 1, :])
    s_near = s_row[...] + p_low[0]
    for copy in low_sends:
        copy.wait_recv()
    s_row[...] = s_near + p_got[1] + p_got[2]

    for g in range(blocks):
        times_rows(
            [(minv.at[g], s_row[g : g + 1, :])], q_col.at[g], q_ext.at[0, g : g + 1, :]
        )
    q_sends = [send(2 * BAND + d - 1, q_ext.at[0], q_ext.at[d], -d) for d in range(1, BAND + 1)]
    for copy in q_sends:
        copy.start()

    near_mine = near_buf.at[mine]

    def put_dot(index, value):
        whole = jnp.sum(value, axis=0, keepdims=True)
        total = whole[:, 0:LANES]
        for low, high in groups[1:]:
            if high - low == LANES:
                total = total + whole[:, low:high]
        near_mine[index : index + 1, :] = total
        low, high = groups[-1]
        if high - low < LANES:
            near_mine[index : index + 1, 0 : high - low] = (
                total[:, 0 : high - low] + whole[:, low:high]
            )

    put_dot(0, rhs[...] * p_ext[0])
    put_dot(1, p_ext[0] * s_row[...])
    put_dot(2, s_row[...] * q_ext[0])

    for g in range(blocks):
        times_columns(
            [tiles.at[g, k] for k in range(slots)],
            q_col.at[g],
            [slot_row(g, k) for k in range(slots)],
        )
    for d in range(1, BAND + 1):
        q_low[d] = spread(d)
    q_low_sends = [
        send(3 * BAND + d - 1, q_low.at[d], q_got.at[d], d) for d in range(1, BAND + 1)
    ]
    for copy in q_low_sends:
        copy.start()
    q_low[0] = spread(0)
    for g in range(blocks):
        w_row[g : g + 1, :] = slot_row(g, 0)[...]
    w_row[...] = w_row[...] + q_low[0]
    own = q_ext[0] * w_row[...]

    for copy in q_sends:
        copy.wait_recv()
    cross = jnp.zeros((1, width), jnp.float32)
    for d in range(1, BAND + 1):
        cross = cross + jnp.sum(q_ext[d] * q_low[d], axis=0, keepdims=True)
    diag = jnp.zeros((1, width), jnp.float32)
    for g in range(blocks):
        diag = diag + slot_row(g, 0)[...] * q_ext[0, g : g + 1, :]
    inner = jnp.sum(own, axis=0, keepdims=True)
    put_dot(3, 2.0 * (cross + inner) - diag)

    near_sends = []
    for d in range(1, NEAR):
        near_sends.append(
            pltpu.make_async_remote_copy(
                src_ref=near_mine,
                dst_ref=near_mine,
                send_sem=near_send.at[d],
                recv_sem=near_recv.at[d],
                device_id=near_peer(d),
                device_id_type=MESH,
            )
        )
    for copy in near_sends:
        copy.start()
    for copy in near_sends:
        copy.wait_recv()
    far_mine = far_buf.at[plane]
    far_mine[...] = jnp.sum(near_buf[...], axis=0)
    far_sends = []
    for d in range(1, far):
        far_sends.append(
            pltpu.make_async_remote_copy(
                src_ref=far_mine,
                dst_ref=far_mine,
                send_sem=far_send.at[d],
                recv_sem=far_recv.at[d],
                device_id=far_peer(d),
                device_id_type=MESH,
            )
        )
    for copy in far_sends:
        copy.start()

    for g in range(blocks):
        terms = [(tiles.at[g, k], picked(q_ext, g, k)) for k in range(1, slots)]
        times_rows(terms, None, s_row_up(prods, g))
    up = prods[0:blocks, :]
    for copy in q_low_sends:
        copy.wait_recv()
    w_row[...] = w_row[...] + up + q_got[1] + q_got[2]

    for copy in far_sends:
        copy.wait_recv()
    sums = jnp.sum(jnp.sum(far_buf[...], axis=0), axis=1, keepdims=True)
    sums = jnp.broadcast_to(sums, (sums.shape[0], width))
    rz, ps, sq, qw = [sums[i : i + 1, :] for i in range(4)]
    alpha = rz / ps
    fresh = rz - 2.0 * alpha * ps + alpha * alpha * sq
    grow = 1.0 + fresh / rz
    energy = grow * grow * ps - 2.0 * grow * alpha * sq + alpha * alpha * qw
    second = fresh / energy
    x_out[...] = (alpha + second * grow) * p_ext[0] - second * alpha * q_ext[0]
    r_out[...] = rhs[...] - (alpha + second * grow) * s_row[...] + second * alpha * w_row[...]

    for copy in p_sends + low_sends + q_sends + q_low_sends + near_sends + far_sends:
        copy.wait_send()


def s_row_up(ref, g):
    return ref.at[g : g + 1, :]


def solution(mesh):
    n = mesh.shape[AXIS]

    def on_device(right_side, schur_tiles, block_cols, tile_counts, jacobi_inverse):
        blocks, slots, width, _ = schur_tiles.shape
        dma = pltpu.SemaphoreType.DMA
        row = jax.ShapeDtypeStruct((blocks, width), jnp.float32)

        def vmem(*shape):
            return pltpu.VMEM(shape, jnp.float32)

        any_spec = pl.BlockSpec(memory_space=pl.ANY)
        vmem_spec = pl.BlockSpec(memory_space=pltpu.VMEM)
        return pl.pallas_call(
            functools.partial(kernel, n),
            out_shape=(row, row),
            in_specs=[any_spec] * 5,
            out_specs=(vmem_spec, vmem_spec),
            scratch_shapes=[
                vmem(blocks, slots, width, width),
                vmem(blocks, width, width),
                vmem(blocks, width),
                pltpu.SMEM((blocks, slots), jnp.int32),
                pltpu.SMEM((blocks,), jnp.int32),
                vmem(blocks, width, LANES),
                vmem(blocks, width, LANES),
                vmem(BAND + 1, blocks, width),
                vmem(BAND + 1, blocks, width),
                vmem(blocks, width),
                vmem(blocks, width),
                vmem(blocks * slots, width),
                vmem(BAND + 1, blocks, width),
                vmem(BAND + 1, blocks, width),
                vmem(BAND + 1, blocks, width),
                vmem(BAND + 1, blocks, width),
                vmem(NEAR, 4, LANES),
                vmem(n // NEAR, 4, LANES),
                dma((blocks * slots,)),
                dma((blocks,)),
                dma((3,)),
                dma((4 * BAND,)),
                dma((4 * BAND,)),
                dma((NEAR,)),
                dma((NEAR,)),
                dma((n // NEAR,)),
                dma((n // NEAR,)),
            ],
            compiler_params=pltpu.CompilerParams(
                collective_id=0, has_side_effects=True, vmem_limit_bytes=60 << 20
            ),
        )(right_side, schur_tiles, block_cols, tile_counts, jacobi_inverse)

    return jax.shard_map(
        on_device,
        mesh=mesh,
        in_specs=(
            P(AXIS, None),
            P(AXIS, None, None, None),
            P(AXIS, None),
            P(AXIS),
            P(AXIS, None, None),
        ),
        out_specs=(P(AXIS, None), P(AXIS, None)),
        check_vma=False,
    )
```

time: 256 us -> 32.8 us (0.13)
  blocking collectives: 195 us -> 0 us
  matrix products: 32.3 us -> 0 us
  Pallas kernels: 0 us -> 29.4 us
  starting transfers between devices: 16.1 us -> 0 us
  other arithmetic: 4.27 us -> 0 us
  between operations: 4.8 us -> 0.64 us
    psum x3 -> x0, blocking collectives: 195 us -> none  [the longest x2 129 us: inner_norm(): return lax.psum(jnp.sum(residual * precond), 'cams')]
    dot_general x8 -> x0, matrix products: 32.3 us -> none  [the longest x2 16.4 us: apply_schur(): upper = jnp.einsum('bsij,bsj->bsi', schur_tiles, picked, precision=HIGH)]
    pallas_call x0 -> x1, Pallas kernels: none -> 29.4 us  [on_device(): pl.pallas_call(functools.partial(kernel, n), out_shape=(row, row), in_spe...]
    ppermute x8 -> x0, starting transfers between devices: 16.1 us -> none  [shifted(): return lax.ppermute(value, axis, pairs)]
  transfers between devices with their start and end apart: 8 -> 0, of which waited for: 0 -> 0; matrix products, arithmetic and copies ran while one was open for 12% -> 0% of each run, Pallas kernels for 0% -> 0%
where the time goes in v1:
time: 32.8 us; the launch traced here: 32.6 us
  Pallas kernels  29.4 us (90%)
  local copies, waits for them, and re-layouts  2.57 us (8%)
  between operations  0.64 us (2%)
    pallas_call x1, Pallas kernels, on_device(): pl.pallas_call(functools.partial(kernel, n), out_shape=(row, row), in_spe...  29.4 us
    unnamed x2, local copies, waits for them, and re-layouts  2.57 us

profile of v1, /device:TPU:1, one launch (start us, length us, event | category | flops | bytes accessed | tf_op | source)
XLA Modules:
  0.0 32.6 jit_solution(2404501714079900278)
XLA Ops:
  0.6 29.4 %shard_map.68 = (f32[4,288]{1,0:T(4,128)}, f32[4,288]{1,0:T(4,128)}) custom-call(f32[4,288]{1,0:T(4,128)} %rhs_hbm.1, f32[4,4,288,288]{3,2,1,0:T(8,128)} %tiles_hbm.1, s32[4,4]{1,0:T(4,128)} %cols_hbm.1, s32[4]{0:T(128)} %counts_hbm.1, f32[4,288,288]{2,1,0:T(8,128)} %minv_hbm.1), custom_call_target="tpu_custom_call" | custom-call | tf_op jit(solution)/shard_map/pallas_call | solution.py:364
  30.1 1.3 %copy.9 = f32[4,288]{1,0:T(4,128)} copy(f32[4,288]{1,0:T(4,128)} %get-tuple-element.4) | data formatting | bytes 9216
  31.4 1.3 %copy.10 = f32[4,288]{1,0:T(4,128)} copy(f32[4,288]{1,0:T(4,128)} %get-tuple-element.5) | data formatting | bytes 9216

commit v2 on v1

--- a/solution.py
+++ b/solution.py
@@ -1,4 +1,5 @@
 import functools
+import itertools
 
 import jax
 import jax.numpy as jnp
@@ -12,6 +13,8 @@
 ROWS = 32
 NEAR = 8
 BAND = 2
+DOTS = 4
+SIZES = {128: (4, 4, 4, 2), 16: (1, 2, 4, 2)}
 AXIS = "cams"
 
 
@@ -22,6 +25,22 @@
 def fold_rows(value):
     rows, width = value.shape
     return jnp.sum(value.reshape(rows // 8, 8, width), axis=0)
+
+
+def all_peers(n, me):
+    sizes = SIZES[n]
+    moved, stride = [], n
+    for size in sizes:
+        stride //= size
+        place = lax.rem(lax.div(me, stride), size)
+        moved.append([lax.rem(place + step, size) * stride for step in range(size)])
+    offsets = list(itertools.product(*[range(size) for size in sizes]))[1:]
+
+    def hops(offset):
+        return sum(min(o, s - o) for o, s in zip(offset[:-1], sizes[:-1])) + 0.1 * offset[-1]
+
+    for offset in sorted(offsets, key=hops, reverse=True):
+        yield sum(axis[step] for axis, step in zip(moved[1:], offset[1:])) + moved[0][offset[0]]
 
 
 def kernel(
@@ -31,8 +50,13 @@
     cols_hbm,
     counts_hbm,
     minv_hbm,
-    x_out,
-    r_out,
+    p_out,
+    q_out,
+    s_out,
+    w_out,
+    rhs_out,
+    one_out,
+    two_out,
     tiles,
     minv,
     rhs,
@@ -49,17 +73,16 @@
     q_low,
     p_got,
     q_got,
-    near_buf,
-    far_buf,
+    dots,
+    everyone,
     tile_sem,
     minv_sem,
     small_sem,
     halo_send,
     halo_recv,
-    near_send,
-    near_recv,
-    far_send,
-    far_recv,
+    all_send,
+    all_recv,
+    ready,
 ):
     blocks, slots, width, _ = tiles.shape
     far = n // NEAR
@@ -89,9 +112,6 @@
         copy.start()
     small[1].start()
     small[2].start()
-    for k in list(range(1, slots)) + [0]:
-        for g in range(blocks):
-            tile_copy[g, k].start()
 
     def ahead(steps):
         return (lax.rem(me + n + steps, n),)
@@ -159,13 +179,22 @@
                 row_out[:, low:high] = jnp.sum(value, axis=0, keepdims=True)
 
     small[0].wait()
-    for g in range(blocks):
-        minv_copy[g].wait()
+    minv_copy[0].wait()
+    for g in range(blocks):
+        for k in range(1, slots):
+            tile_copy[g, k].start()
+    for g in range(blocks):
+        tile_copy[g, 0].start()
+    for g in range(blocks):
+        if g > 0:
+            minv_copy[g].wait()
         times_rows(
             [(minv.at[g], rhs[g : g + 1, :])], p_col.at[g], p_ext.at[0, g : g + 1, :]
         )
 
     pl.semaphore_wait(barrier, len(peers))
+    for d in range(1, NEAR):
+        pl.semaphore_signal(ready, inc=1, device_id=near_peer(d), device_id_type=MESH)
     p_sends = [send(d - 1, p_ext.at[0], p_ext.at[d], -d) for d in range(1, BAND + 1)]
     for copy in p_sends:
         copy.start()
@@ -237,20 +266,9 @@
     for copy in q_sends:
         copy.start()
 
-    near_mine = near_buf.at[mine]
-
     def put_dot(index, value):
-        whole = jnp.sum(value, axis=0, keepdims=True)
-        total = whole[:, 0:LANES]
-        for low, high in groups[1:]:
-            if high - low == LANES:
-                total = total + whole[:, low:high]
-        near_mine[index : index + 1, :] = total
-        low, high = groups[-1]
-        if high - low < LANES:
-            near_mine[index : index + 1, 0 : high - low] = (
-                total[:, 0 : high - low] + whole[:, low:high]
-            )
+        whole = jnp.sum(jnp.sum(value, axis=0, keepdims=True), axis=1, keepdims=True)
+        dots[index : index + 1, :] = jnp.broadcast_to(whole, (1, LANES))
 
     put_dot(0, rhs[...] * p_ext[0])
     put_dot(1, p_ext[0] * s_row[...])
@@ -286,39 +304,27 @@
     inner = jnp.sum(own, axis=0, keepdims=True)
     put_dot(3, 2.0 * (cross + inner) - diag)
 
-    near_sends = []
-    for d in range(1, NEAR):
-        near_sends.append(
-            pltpu.make_async_remote_copy(
-                src_ref=near_mine,
-                dst_ref=near_mine,
-                send_sem=near_send.at[d],
-                recv_sem=near_recv.at[d],
-                device_id=near_peer(d),
-                device_id_type=MESH,
-            )
-        )
-    for copy in near_sends:
-        copy.start()
-    for copy in near_sends:
-        copy.wait_recv()
-    far_mine = far_buf.at[plane]
-    far_mine[...] = jnp.sum(near_buf[...], axis=0)
-    far_sends = []
-    for d in range(1, far):
-        far_sends.append(
-            pltpu.make_async_remote_copy(
-                src_ref=far_mine,
-                dst_ref=far_mine,
-                send_sem=far_send.at[d],
-                recv_sem=far_recv.at[d],
-                device_id=far_peer(d),
-                device_id_type=MESH,
-            )
-        )
-    for copy in far_sends:
-        copy.start()
-
+    lane = lax.broadcasted_iota(jnp.int32, (1, LANES), 1)
+    mixed = dots[0:1, :]
+    for index in range(1, DOTS):
+        mixed = jnp.where(lane < index * (LANES // DOTS), mixed, dots[index : index + 1, :])
+    everyone[me] = mixed
+    pl.semaphore_wait(ready, NEAR - 1)
+    for peer in all_peers(n, me):
+        pltpu.make_async_remote_copy(
+            src_ref=everyone.at[me],
+            dst_ref=everyone.at[me],
+            send_sem=all_send,
+            recv_sem=all_recv,
+            device_id=(peer,),
+            device_id_type=MESH,
+        ).start()
+    others = everyone.at[pl.ds(0, n - 1)]
+
+    p_out[...] = p_ext[0]
+    q_out[...] = q_ext[0]
+    s_out[...] = s_row[...]
+    rhs_out[...] = rhs[...]
     for g in range(blocks):
         terms = [(tiles.at[g, k], picked(q_ext, g, k)) for k in range(1, slots)]
         times_rows(terms, None, s_row_up(prods, g))
@@ -327,21 +333,27 @@
         copy.wait_recv()
     w_row[...] = w_row[...] + up + q_got[1] + q_got[2]
 
-    for copy in far_sends:
-        copy.wait_recv()
-    sums = jnp.sum(jnp.sum(far_buf[...], axis=0), axis=1, keepdims=True)
-    sums = jnp.broadcast_to(sums, (sums.shape[0], width))
-    rz, ps, sq, qw = [sums[i : i + 1, :] for i in range(4)]
+    pltpu.make_async_copy(others, others, all_recv).wait()
+    sums = jnp.sum(everyone[...], axis=0)
+
+    def dot(index):
+        first = lane == index * (LANES // DOTS)
+        total = jnp.sum(jnp.where(first, sums, 0.0), axis=1, keepdims=True)
+        return jnp.broadcast_to(total, (blocks, width))
+
+    rz, ps, sq, qw = [dot(index) for index in range(DOTS)]
     alpha = rz / ps
     fresh = rz - 2.0 * alpha * ps + alpha * alpha * sq
     grow = 1.0 + fresh / rz
     energy = grow * grow * ps - 2.0 * grow * alpha * sq + alpha * alpha * qw
     second = fresh / energy
-    x_out[...] = (alpha + second * grow) * p_ext[0] - second * alpha * q_ext[0]
-    r_out[...] = rhs[...] - (alpha + second * grow) * s_row[...] + second * alpha * w_row[...]
-
-    for copy in p_sends + low_sends + q_sends + q_low_sends + near_sends + far_sends:
+    one_out[...] = alpha + second * grow
+    two_out[...] = second * alpha
+    w_out[...] = w_row[...]
+
+    for copy in p_sends + low_sends + q_sends + q_low_sends:
         copy.wait_send()
+    pltpu.make_async_copy(others, others, all_send).wait()
 
 
 def s_row_up(ref, g):
@@ -354,18 +366,17 @@
     def on_device(right_side, schur_tiles, block_cols, tile_counts, jacobi_inverse):
         blocks, slots, width, _ = schur_tiles.shape
         dma = pltpu.SemaphoreType.DMA
-        row = jax.ShapeDtypeStruct((blocks, width), jnp.float32)
 
         def vmem(*shape):
             return pltpu.VMEM(shape, jnp.float32)
 
         any_spec = pl.BlockSpec(memory_space=pl.ANY)
         vmem_spec = pl.BlockSpec(memory_space=pltpu.VMEM)
-        return pl.pallas_call(
+        p, q, s, w, rhs, one, two = pl.pallas_call(
             functools.partial(kernel, n),
-            out_shape=(row, row),
+            out_shape=[vmem(blocks, width)] * 7,
             in_specs=[any_spec] * 5,
-            out_specs=(vmem_spec, vmem_spec),
+            out_specs=[vmem_spec] * 7,
             scratch_shapes=[
                 vmem(blocks, slots, width, width),
                 vmem(blocks, width, width),
@@ -383,22 +394,22 @@
                 vmem(BAND + 1, blocks, width),
                 vmem(BAND + 1, blocks, width),
                 vmem(BAND + 1, blocks, width),
-                vmem(NEAR, 4, LANES),
-                vmem(n // NEAR, 4, LANES),
+                vmem(DOTS, LANES),
+                vmem(n, 1, LANES),
                 dma((blocks * slots,)),
                 dma((blocks,)),
                 dma((3,)),
                 dma((4 * BAND,)),
                 dma((4 * BAND,)),
-                dma((NEAR,)),
-                dma((NEAR,)),
-                dma((n // NEAR,)),
-                dma((n // NEAR,)),
+                dma(()),
+                dma(()),
+                pltpu.SemaphoreType.REGULAR,
             ],
             compiler_params=pltpu.CompilerParams(
                 collective_id=0, has_side_effects=True, vmem_limit_bytes=60 << 20
             ),
         )(right_side, schur_tiles, block_cols, tile_counts, jacobi_inverse)
+        return one * p - two * q, rhs - one * s + two * w
 
     return jax.shard_map(
         on_device,

time: 32.8 us -> 28.1 us (0.86)
  Pallas kernels: 29.4 us -> 26.8 us
  local copies, waits for them, and re-layouts: 2.57 us -> 0 us
  other arithmetic: 0 us -> 0.61 us
    pallas_call x1, Pallas kernels: 29.4 us -> 26.8 us  [on_device(): pl.pallas_call(functools.partial(kernel, n), out_shape=[vmem(blocks, widt...]
    unnamed x2 -> x0, local copies, waits for them, and re-layouts: 2.57 us -> none
    add x0 -> x1, other arithmetic: none -> 0.61 us  [on_device(): return (one * p - two * q, rhs - one * s + two * w)]
where the time goes in v2:
time: 28.1 us; the launch traced here: 28 us
  Pallas kernels  26.8 us (95%)
  between operations  0.64 us (2%)
  other arithmetic  0.61 us (2%)
    pallas_call x1, Pallas kernels, on_device(): pl.pallas_call(functools.partial(kernel, n), out_shape=[vmem(blocks, widt...  26.8 us
    add x1, other arithmetic, on_device(): return (one * p - two * q, rhs - one * s + two * w)  0.61 us

profile of v2, /device:TPU:1, one launch (start us, length us, event | category | flops | bytes accessed | tf_op | source)
XLA Modules:
  0.0 28.0 jit_solution(14459486401435511531)
XLA Ops:
  0.6 26.8 %shard_map.68 = (f32[4,288]{1,0:T(4,128)S(1)}, f32[4,288]{1,0:T(4,128)S(1)}, f32[4,288]{1,0:T(4,128)S(1)}, f32[4,288]{1,0:T(4,128)S(1)}, f32[4,288]{1,0:T(4,128)...) custom-call(f32[4,288]{1,0:T(4,128)} %rhs_hbm.1, f32[4,4,288,288]{3,2,1,0:T(8,128)} %tiles_hbm.1, s32[4,4]{1,0:T(4,128)} %cols_hbm.1, ...), custom_call_target="tpu_custom_call" | custom-call | tf_op jit(solution)/shard_map/pallas_call | solution.py:375
  27.4 0.6 %multiply_add_fusion = (f32[4,288]{1,0:T(4,128)}, f32[4,288]{1,0:T(4,128)}) fusion(f32[4,288]{1,0:T(4,128)S(1)} %get-tuple-element.11, f32[4,288]{1,0:T(4,128)S(1)} %get-tuple-element.15, f32[4,288]{1,0:T(4,128)S(1)} %get-tuple-element.13, f32[4,288]{1,0:T(4,128)S(1)} %get-tuple-element.9, f32[4,288]{1,0:T(4,128)S(1)} %get-tuple-element.14, ...), kind=kLoop, calls=%fused_computation | loop fusion | flops 8064 | bytes 41472 | tf_op jit(solution)/shard_map/add | solution.py:412

commit v3 on v2

--- a/solution.py
+++ b/solution.py
@@ -25,6 +25,43 @@
 def fold_rows(value):
     rows, width = value.shape
     return jnp.sum(value.reshape(rows // 8, 8, width), axis=0)
+
+
+def two_sum(a, b):
+    total = a + b
+    part = total - a
+    return total, (a - (total - part)) + (b - part)
+
+
+def split(a):
+    wide = 4097.0 * a
+    high = wide - (wide - a)
+    return high, a - high
+
+
+def two_product(a, b):
+    product = a * b
+    a_high, a_low = split(a)
+    b_high, b_low = split(b)
+    error = ((a_high * b_high - product) + a_high * b_low + a_low * b_high) + a_low * b_low
+    return product, error
+
+
+def sum_pairs(ref):
+    parts = [(ref[at : at + 8, :], None) for at in range(0, ref.shape[0], 8)]
+
+    def add(first, second):
+        total, error = two_sum(first[0], second[0])
+        for extra in (first[1], second[1]):
+            error = error if extra is None else error + extra
+        return total, error
+
+    while len(parts) > 1:
+        parts = [add(parts[i], parts[i + 1]) for i in range(0, len(parts), 2)]
+    part = parts[0]
+    for shift in (4, 2, 1):
+        part = add(part, tuple(pltpu.roll(half, shift, 0) for half in part))
+    return part[0][0:1, :], part[1][0:1, :]
 
 
 def all_peers(n, me):
@@ -74,12 +111,17 @@
     p_got,
     q_got,
     dots,
+    cross,
+    mid_q,
+    mid_low,
     everyone,
     tile_sem,
     minv_sem,
     small_sem,
     halo_send,
     halo_recv,
+    mid_send,
+    mid_recv,
     all_send,
     all_recv,
     ready,
@@ -247,13 +289,14 @@
 
     for g in range(blocks):
         tile_copy[g, 0].wait()
+        times_columns([tiles.at[g, 0]], p_col.at[g], [w_row.at[g : g + 1, :]])
+    w_row[...] = w_row[...] + p_low[0]
     for copy in p_sends:
         copy.wait_recv()
     for g in range(blocks):
-        terms = [(tiles.at[g, 0], p_ext[0, g : g + 1, :])]
-        terms += [(tiles.at[g, k], picked(p_ext, g, k)) for k in range(1, slots)]
+        terms = [(tiles.at[g, k], picked(p_ext, g, k)) for k in range(1, slots)]
         times_rows(terms, None, s_row.at[g : g + 1, :])
-    s_near = s_row[...] + p_low[0]
+    s_near = s_row[...] + w_row[...]
     for copy in low_sends:
         copy.wait_recv()
     s_row[...] = s_near + p_got[1] + p_got[2]
@@ -266,6 +309,29 @@
     for copy in q_sends:
         copy.start()
 
+    def halfway(index, source, target, peer):
+        return pltpu.make_async_remote_copy(
+            src_ref=source,
+            dst_ref=target,
+            send_sem=mid_send.at[index],
+            recv_sem=mid_recv.at[index],
+            device_id=peer,
+            device_id_type=MESH,
+        )
+
+    def halfway_q():
+        return halfway(0, q_ext.at[0], mid_q, ahead(-NEAR))
+
+    def halfway_low(distance, place):
+        return halfway(
+            distance, q_low.at[distance], mid_low.at[distance], (plane * NEAR + place,)
+        )
+
+    @pl.when(mine < BAND)
+    def _():
+        halfway_q().start()
+
+
     def put_dot(index, value):
         whole = jnp.sum(jnp.sum(value, axis=0, keepdims=True), axis=1, keepdims=True)
         dots[index : index + 1, :] = jnp.broadcast_to(whole, (1, LANES))
@@ -276,12 +342,22 @@
 
     for g in range(blocks):
         times_columns(
-            [tiles.at[g, k] for k in range(slots)],
+            [tiles.at[g, k] for k in range(1, slots)],
             q_col.at[g],
-            [slot_row(g, k) for k in range(slots)],
+            [slot_row(g, k) for k in range(1, slots)],
         )
     for d in range(1, BAND + 1):
         q_low[d] = spread(d)
+
+    @pl.when(mine == NEAR - 1)
+    def _():
+        halfway_low(1, 0).start()
+        halfway_low(2, 1).start()
+
+    @pl.when(mine == NEAR - 2)
+    def _():
+        halfway_low(2, 0).start()
+
     q_low_sends = [
         send(3 * BAND + d - 1, q_low.at[d], q_got.at[d], d) for d in range(1, BAND + 1)
     ]
@@ -289,42 +365,68 @@
         copy.start()
     q_low[0] = spread(0)
     for g in range(blocks):
-        w_row[g : g + 1, :] = slot_row(g, 0)[...]
+        times_columns([tiles.at[g, 0]], q_col.at[g], [w_row.at[g : g + 1, :]])
+    cross[...] = jnp.sum(
+        q_ext[0] * (2.0 * q_low[0] + w_row[...]), axis=0, keepdims=True
+    )
     w_row[...] = w_row[...] + q_low[0]
-    own = q_ext[0] * w_row[...]
-
-    for copy in q_sends:
-        copy.wait_recv()
-    cross = jnp.zeros((1, width), jnp.float32)
-    for d in range(1, BAND + 1):
-        cross = cross + jnp.sum(q_ext[d] * q_low[d], axis=0, keepdims=True)
-    diag = jnp.zeros((1, width), jnp.float32)
-    for g in range(blocks):
-        diag = diag + slot_row(g, 0)[...] * q_ext[0, g : g + 1, :]
-    inner = jnp.sum(own, axis=0, keepdims=True)
-    put_dot(3, 2.0 * (cross + inner) - diag)
-
+
+    def add_cross(rows, low):
+        cross[...] = cross[...] + 2.0 * jnp.sum(rows * low, axis=0, keepdims=True)
+
+    @pl.when(mine < NEAR - 1)
+    def _():
+        q_sends[0].wait_recv()
+        add_cross(q_ext[1], q_low[1])
+
+    @pl.when(mine < NEAR - 2)
+    def _():
+        q_sends[1].wait_recv()
+        add_cross(q_ext[2], q_low[2])
+
+    @pl.when(mine == 0)
+    def _():
+        halfway_q().wait_recv()
+        halfway_low(1, 0).wait_recv()
+        halfway_low(2, 0).wait_recv()
+        add_cross(mid_q[...], mid_low[1] + mid_low[2])
+
+    @pl.when(mine == 1)
+    def _():
+        halfway_q().wait_recv()
+        halfway_low(2, 0).wait_recv()
+        add_cross(mid_q[...], mid_low[2])
+
+    put_dot(3, cross[...])
     lane = lax.broadcasted_iota(jnp.int32, (1, LANES), 1)
     mixed = dots[0:1, :]
     for index in range(1, DOTS):
         mixed = jnp.where(lane < index * (LANES // DOTS), mixed, dots[index : index + 1, :])
-    everyone[me] = mixed
+    everyone[pl.ds(me, 1), :] = mixed
     pl.semaphore_wait(ready, NEAR - 1)
     for peer in all_peers(n, me):
         pltpu.make_async_remote_copy(
-            src_ref=everyone.at[me],
-            dst_ref=everyone.at[me],
+            src_ref=everyone.at[pl.ds(me, 1), :],
+            dst_ref=everyone.at[pl.ds(me, 1), :],
             send_sem=all_send,
             recv_sem=all_recv,
             device_id=(peer,),
             device_id_type=MESH,
         ).start()
-    others = everyone.at[pl.ds(0, n - 1)]
+    others = everyone.at[pl.ds(0, n - 1), :]
 
     p_out[...] = p_ext[0]
     q_out[...] = q_ext[0]
     s_out[...] = s_row[...]
     rhs_out[...] = rhs[...]
+    @pl.when(mine >= NEAR - 1)
+    def _():
+        q_sends[0].wait_recv()
+
+    @pl.when(mine >= NEAR - 2)
+    def _():
+        q_sends[1].wait_recv()
+
     for g in range(blocks):
         terms = [(tiles.at[g, k], picked(q_ext, g, k)) for k in range(1, slots)]
         times_rows(terms, None, s_row_up(prods, g))
@@ -334,26 +436,48 @@
     w_row[...] = w_row[...] + up + q_got[1] + q_got[2]
 
     pltpu.make_async_copy(others, others, all_recv).wait()
-    sums = jnp.sum(everyone[...], axis=0)
+    high, low = sum_pairs(everyone)
 
     def dot(index):
         first = lane == index * (LANES // DOTS)
-        total = jnp.sum(jnp.where(first, sums, 0.0), axis=1, keepdims=True)
-        return jnp.broadcast_to(total, (blocks, width))
-
-    rz, ps, sq, qw = [dot(index) for index in range(DOTS)]
-    alpha = rz / ps
-    fresh = rz - 2.0 * alpha * ps + alpha * alpha * sq
-    grow = 1.0 + fresh / rz
-    energy = grow * grow * ps - 2.0 * grow * alpha * sq + alpha * alpha * qw
-    second = fresh / energy
-    one_out[...] = alpha + second * grow
-    two_out[...] = second * alpha
+        return [
+            jnp.sum(jnp.where(first, part, 0.0), axis=1, keepdims=True) for part in (high, low)
+        ]
+
+    (rz, rz_low), (ps, ps_low), (sq, sq_low), (qw, qw_low) = [dot(i) for i in range(DOTS)]
+
+    def ratio(top, top_low):
+        value = top / ps
+        product, error = two_product(value, ps)
+        return value, ((top - product) - error + (top_low - value * ps_low)) / ps
+
+    alpha, alpha_low = ratio(rz, rz_low)
+    gamma, gamma_low = ratio(sq, sq_low)
+    product, error = two_product(alpha, sq)
+    upper = (product - ps) + (error + (alpha * sq_low - ps_low) + alpha_low * sq)
+    product, error = two_product(gamma, sq)
+    lower = (qw - product) - (error - qw_low + gamma * sq_low + gamma_low * sq)
+    two = upper / lower
+    one = alpha + two * gamma
+    one_out[...] = jnp.broadcast_to(one, (blocks, width))
+    two_out[...] = jnp.broadcast_to(two, (blocks, width))
     w_out[...] = w_row[...]
 
     for copy in p_sends + low_sends + q_sends + q_low_sends:
         copy.wait_send()
     pltpu.make_async_copy(others, others, all_send).wait()
+
+    @pl.when(mine < BAND)
+    def _():
+        halfway_q().wait_send()
+
+    @pl.when(mine == NEAR - 1)
+    def _():
+        halfway_low(1, 0).wait_send()
+
+    @pl.when(mine >= NEAR - 2)
+    def _():
+        halfway_low(2, 0).wait_send()
 
 
 def s_row_up(ref, g):
@@ -395,12 +519,17 @@
                 vmem(BAND + 1, blocks, width),
                 vmem(BAND + 1, blocks, width),
                 vmem(DOTS, LANES),
-                vmem(n, 1, LANES),
+                vmem(1, width),
+                vmem(blocks, width),
+                vmem(BAND + 1, blocks, width),
+                vmem(n, LANES),
                 dma((blocks * slots,)),
                 dma((blocks,)),
                 dma((3,)),
                 dma((4 * BAND,)),
                 dma((4 * BAND,)),
+                dma((BAND + 1,)),
+                dma((BAND + 1,)),
                 dma(()),
                 dma(()),
                 pltpu.SemaphoreType.REGULAR,

time: 28.1 us -> 26.4 us (0.940)
  Pallas kernels: 26.8 us -> 25 us
    pallas_call x1, Pallas kernels: 26.8 us -> 25 us  [on_device(): pl.pallas_call(functools.partial(kernel, n), out_shape=[vmem(blocks, widt...]
where the time goes in v3:
time: 26.4 us; the launch traced here: 26.3 us
  Pallas kernels  25 us (95%)
  between operations  0.64 us (2%)
  other arithmetic  0.61 us (2%)
    pallas_call x1, Pallas kernels, on_device(): pl.pallas_call(functools.partial(kernel, n), out_shape=[vmem(blocks, widt...  25 us
    add x1, other arithmetic, on_device(): return (one * p - two * q, rhs - one * s + two * w)  0.61 us

profile of v3, /device:TPU:1, one launch (start us, length us, event | category | flops | bytes accessed | tf_op | source)
XLA Modules:
  0.0 26.3 jit_solution(14923976128949846546)
XLA Ops:
  0.6 25.0 %shard_map.68 = (f32[4,288]{1,0:T(4,128)S(1)}, f32[4,288]{1,0:T(4,128)S(1)}, f32[4,288]{1,0:T(4,128)S(1)}, f32[4,288]{1,0:T(4,128)S(1)}, f32[4,288]{1,0:T(4,128)...) custom-call(f32[4,288]{1,0:T(4,128)} %rhs_hbm.1, f32[4,4,288,288]{3,2,1,0:T(8,128)} %tiles_hbm.1, s32[4,4]{1,0:T(4,128)} %cols_hbm.1, ...), custom_call_target="tpu_custom_call" | custom-call | tf_op jit(solution)/shard_map/pallas_call | solution.py:499
  25.7 0.6 %multiply_add_fusion = (f32[4,288]{1,0:T(4,128)}, f32[4,288]{1,0:T(4,128)}) fusion(f32[4,288]{1,0:T(4,128)S(1)} %get-tuple-element.11, f32[4,288]{1,0:T(4,128)S(1)} %get-tuple-element.15, f32[4,288]{1,0:T(4,128)S(1)} %get-tuple-element.13, f32[4,288]{1,0:T(4,128)S(1)} %get-tuple-element.9, f32[4,288]{1,0:T(4,128)S(1)} %get-tuple-element.14, ...), kind=kLoop, calls=%fused_computation | loop fusion | flops 8064 | bytes 41472 | tf_op jit(solution)/shard_map/add | solution.py:541

commit v4 on v3

--- a/solution.py
+++ b/solution.py
@@ -76,7 +76,7 @@
     def hops(offset):
         return sum(min(o, s - o) for o, s in zip(offset[:-1], sizes[:-1])) + 0.1 * offset[-1]
 
-    for offset in sorted(offsets, key=hops, reverse=True):
+    for offset in sorted(offsets, key=hops):
         yield sum(axis[step] for axis, step in zip(moved[1:], offset[1:])) + moved[0][offset[0]]
 
 
@@ -112,8 +112,7 @@
     q_got,
     dots,
     cross,
-    mid_q,
-    mid_low,
+    mid_p,
     everyone,
     tile_sem,
     minv_sem,
@@ -149,11 +148,14 @@
         for g in range(blocks)
         for k in range(slots)
     }
+    def start_tiles(g):
+        for k in range(1, slots):
+            tile_copy[g, k].start()
+
     small[0].start()
     for copy in minv_copy:
         copy.start()
-    small[1].start()
-    small[2].start()
+    start_tiles(0)
 
     def ahead(steps):
         return (lax.rem(me + n + steps, n),)
@@ -164,12 +166,50 @@
     def far_peer(steps):
         return (lax.rem(plane + far + steps, far) * NEAR + mine,)
 
+    def ring_peers(axis):
+        size = SIZES[n][axis]
+        stride = 1 if axis == 1 else SIZES[n][1]
+        place = lax.rem(lax.div(plane, stride), size)
+        for step in range(1, size):
+            moved = plane + (lax.rem(place + step, size) - place) * stride
+            yield (moved * NEAR + mine,)
+
+    line = lax.rem(plane, SIZES[n][1])
+    first = line == 0
+    last = line == SIZES[n][1] - 1
+    relayed = first & (mine < BAND)
+
     barrier = pltpu.get_barrier_semaphore()
-    peers = [ahead(s) for s in (1, -1, 2, -2)]
-    peers += [near_peer(s) for s in range(1, NEAR)]
-    peers += [far_peer(s) for s in range(1, far)]
+
+    def enter(peer):
+        pl.semaphore_signal(barrier, inc=1, device_id=peer, device_id_type=MESH)
+
+    @pl.when(mine == 0)
+    def _():
+        enter(ahead(-1))
+
+    @pl.when(mine < BAND)
+    def _():
+        enter(ahead(-2))
+
+    @pl.when(last & (mine < BAND))
+    def _():
+        enter(ahead(NEAR))
+
+    @pl.when(jnp.logical_not(last) & (mine >= NEAR - 2))
+    def _():
+        enter(ahead(2))
+
+    @pl.when(jnp.logical_not(last) & (mine == NEAR - 1))
+    def _():
+        enter(ahead(1))
+
+    peers = [near_peer(s) for s in range(1, NEAR)]
+    peers += [*ring_peers(0), *ring_peers(1)]
     for peer in peers:
-        pl.semaphore_signal(barrier, inc=1, device_id=peer, device_id_type=MESH)
+        enter(peer)
+    links = jnp.where(mine == 0, jnp.where(first, 1, 2), 0) + jnp.where(mine == 1, 1, 0)
+    links = links + jnp.where(mine == NEAR - 2, 1, 0) + jnp.where(mine == NEAR - 1, 2, 0)
 
     def send(index, source, target, steps):
         return pltpu.make_async_remote_copy(
@@ -220,26 +260,56 @@
             for (low, high), value in zip(groups, sums[index]):
                 row_out[:, low:high] = jnp.sum(value, axis=0, keepdims=True)
 
+    start_tiles(1)
+    small[1].start()
+    small[2].start()
     small[0].wait()
-    minv_copy[0].wait()
-    for g in range(blocks):
-        for k in range(1, slots):
-            tile_copy[g, k].start()
-    for g in range(blocks):
-        tile_copy[g, 0].start()
-    for g in range(blocks):
-        if g > 0:
-            minv_copy[g].wait()
+    for g in range(blocks):
+        minv_copy[g].wait()
+        if g + 2 < blocks:
+            start_tiles(g + 2)
         times_rows(
             [(minv.at[g], rhs[g : g + 1, :])], p_col.at[g], p_ext.at[0, g : g + 1, :]
         )
 
-    pl.semaphore_wait(barrier, len(peers))
-    for d in range(1, NEAR):
-        pl.semaphore_signal(ready, inc=1, device_id=near_peer(d), device_id_type=MESH)
+    pl.semaphore_wait(barrier, len(peers) + links)
     p_sends = [send(d - 1, p_ext.at[0], p_ext.at[d], -d) for d in range(1, BAND + 1)]
-    for copy in p_sends:
-        copy.start()
+
+    def relay(index, source, target, recv, peer):
+        return pltpu.make_async_remote_copy(
+            src_ref=source,
+            dst_ref=target,
+            send_sem=mid_send.at[index],
+            recv_sem=recv,
+            device_id=peer,
+            device_id_type=MESH,
+        )
+
+    def relay_in():
+        return relay(0, p_ext.at[0], mid_p, mid_recv, ahead(-NEAR))
+
+    def relay_out(distance, place):
+        return relay(
+            distance,
+            mid_p,
+            p_ext.at[distance],
+            halo_recv.at[distance - 1],
+            (plane * NEAR + place,),
+        )
+
+    @pl.when(relayed)
+    def _():
+        relay_in().start()
+
+    direct = [jnp.logical_not(first & (mine < d)) for d in range(1, BAND + 1)]
+    for copy, sent in zip(p_sends, direct):
+
+        @pl.when(sent)
+        def _(copy=copy):
+            copy.start()
+
+    for peer in ring_peers(1):
+        pl.semaphore_signal(ready.at[0], inc=1, device_id=peer, device_id_type=MESH)
 
     small[1].wait()
     small[2].wait()
@@ -275,6 +345,7 @@
     for g in range(blocks):
         for k in range(1, slots):
             tile_copy[g, k].wait()
+        tile_copy[g, 0].start()
         times_columns(
             [tiles.at[g, k] for k in range(1, slots)],
             p_col.at[g],
@@ -287,16 +358,30 @@
         copy.start()
     p_low[0] = spread(0)
 
+    @pl.when(last & (mine == 0))
+    def _():
+        relay_in().wait_recv()
+        relay_out(1, NEAR - 1).start()
+        relay_out(2, NEAR - 2).start()
+
+    @pl.when(last & (mine == 1))
+    def _():
+        relay_in().wait_recv()
+        relay_out(2, NEAR - 1).start()
+
+    for copy in p_sends:
+        copy.wait_recv()
+    for g in range(blocks):
+        terms = [(tiles.at[g, k], picked(p_ext, g, k)) for k in range(1, slots)]
+        times_rows(terms, None, s_row.at[g : g + 1, :])
     for g in range(blocks):
         tile_copy[g, 0].wait()
         times_columns([tiles.at[g, 0]], p_col.at[g], [w_row.at[g : g + 1, :]])
     w_row[...] = w_row[...] + p_low[0]
-    for copy in p_sends:
-        copy.wait_recv()
-    for g in range(blocks):
-        terms = [(tiles.at[g, k], picked(p_ext, g, k)) for k in range(1, slots)]
-        times_rows(terms, None, s_row.at[g : g + 1, :])
     s_near = s_row[...] + w_row[...]
+    pl.semaphore_wait(ready.at[0], SIZES[n][1] - 1)
+    for d in range(1, NEAR):
+        pl.semaphore_signal(ready.at[1], inc=1, device_id=near_peer(d), device_id_type=MESH)
     for copy in low_sends:
         copy.wait_recv()
     s_row[...] = s_near + p_got[1] + p_got[2]
@@ -308,29 +393,6 @@
     q_sends = [send(2 * BAND + d - 1, q_ext.at[0], q_ext.at[d], -d) for d in range(1, BAND + 1)]
     for copy in q_sends:
         copy.start()
-
-    def halfway(index, source, target, peer):
-        return pltpu.make_async_remote_copy(
-            src_ref=source,
-            dst_ref=target,
-            send_sem=mid_send.at[index],
-            recv_sem=mid_recv.at[index],
-            device_id=peer,
-            device_id_type=MESH,
-        )
-
-    def halfway_q():
-        return halfway(0, q_ext.at[0], mid_q, ahead(-NEAR))
-
-    def halfway_low(distance, place):
-        return halfway(
-            distance, q_low.at[distance], mid_low.at[distance], (plane * NEAR + place,)
-        )
-
-    @pl.when(mine < BAND)
-    def _():
-        halfway_q().start()
-
 
     def put_dot(index, value):
         whole = jnp.sum(jnp.sum(value, axis=0, keepdims=True), axis=1, keepdims=True)
@@ -348,15 +410,6 @@
         )
     for d in range(1, BAND + 1):
         q_low[d] = spread(d)
-
-    @pl.when(mine == NEAR - 1)
-    def _():
-        halfway_low(1, 0).start()
-        halfway_low(2, 1).start()
-
-    @pl.when(mine == NEAR - 2)
-    def _():
-        halfway_low(2, 0).start()
 
     q_low_sends = [
         send(3 * BAND + d - 1, q_low.at[d], q_got.at[d], d) for d in range(1, BAND + 1)
@@ -374,28 +427,23 @@
     def add_cross(rows, low):
         cross[...] = cross[...] + 2.0 * jnp.sum(rows * low, axis=0, keepdims=True)
 
-    @pl.when(mine < NEAR - 1)
-    def _():
-        q_sends[0].wait_recv()
-        add_cross(q_ext[1], q_low[1])
-
-    @pl.when(mine < NEAR - 2)
-    def _():
-        q_sends[1].wait_recv()
-        add_cross(q_ext[2], q_low[2])
-
-    @pl.when(mine == 0)
-    def _():
-        halfway_q().wait_recv()
-        halfway_low(1, 0).wait_recv()
-        halfway_low(2, 0).wait_recv()
-        add_cross(mid_q[...], mid_low[1] + mid_low[2])
-
-    @pl.when(mine == 1)
-    def _():
-        halfway_q().wait_recv()
-        halfway_low(2, 0).wait_recv()
-        add_cross(mid_q[...], mid_low[2])
+    here = [(mine < NEAR - 3) | (mine == NEAR - 2), mine < NEAR - 4]
+    both_there = (mine == 0) | (mine == NEAR - 2)
+    one_there = (mine == 1) | (mine == NEAR - 1)
+    got_there = [both_there, both_there | one_there]
+    for copy, wanted, d in zip(q_sends, here, range(1, BAND + 1)):
+
+        @pl.when(wanted)
+        def _(copy=copy, d=d):
+            copy.wait_recv()
+            add_cross(q_ext[d], q_low[d])
+
+    for copy, wanted, d in zip(q_low_sends, got_there, range(1, BAND + 1)):
+
+        @pl.when(wanted)
+        def _(copy=copy, d=d):
+            copy.wait_recv()
+            add_cross(q_ext[0], q_got[d])
 
     put_dot(3, cross[...])
     lane = lax.broadcasted_iota(jnp.int32, (1, LANES), 1)
@@ -403,7 +451,7 @@
     for index in range(1, DOTS):
         mixed = jnp.where(lane < index * (LANES // DOTS), mixed, dots[index : index + 1, :])
     everyone[pl.ds(me, 1), :] = mixed
-    pl.semaphore_wait(ready, NEAR - 1)
+    pl.semaphore_wait(ready.at[1], NEAR - 1)
     for peer in all_peers(n, me):
         pltpu.make_async_remote_copy(
             src_ref=everyone.at[pl.ds(me, 1), :],
@@ -419,20 +467,22 @@
     q_out[...] = q_ext[0]
     s_out[...] = s_row[...]
     rhs_out[...] = rhs[...]
-    @pl.when(mine >= NEAR - 1)
-    def _():
-        q_sends[0].wait_recv()
-
-    @pl.when(mine >= NEAR - 2)
-    def _():
-        q_sends[1].wait_recv()
+    for copy, wanted in zip(q_sends, here):
+
+        @pl.when(jnp.logical_not(wanted))
+        def _(copy=copy):
+            copy.wait_recv()
 
     for g in range(blocks):
         terms = [(tiles.at[g, k], picked(q_ext, g, k)) for k in range(1, slots)]
         times_rows(terms, None, s_row_up(prods, g))
     up = prods[0:blocks, :]
-    for copy in q_low_sends:
-        copy.wait_recv()
+    for copy, wanted in zip(q_low_sends, got_there):
+
+        @pl.when(jnp.logical_not(wanted))
+        def _(copy=copy):
+            copy.wait_recv()
+
     w_row[...] = w_row[...] + up + q_got[1] + q_got[2]
 
     pltpu.make_async_copy(others, others, all_recv).wait()
@@ -463,21 +513,28 @@
     two_out[...] = jnp.broadcast_to(two, (blocks, width))
     w_out[...] = w_row[...]
 
-    for copy in p_sends + low_sends + q_sends + q_low_sends:
+    for copy in low_sends + q_sends + q_low_sends:
         copy.wait_send()
     pltpu.make_async_copy(others, others, all_send).wait()
 
-    @pl.when(mine < BAND)
-    def _():
-        halfway_q().wait_send()
-
-    @pl.when(mine == NEAR - 1)
-    def _():
-        halfway_low(1, 0).wait_send()
-
-    @pl.when(mine >= NEAR - 2)
-    def _():
-        halfway_low(2, 0).wait_send()
+    for copy, sent in zip(p_sends, direct):
+
+        @pl.when(sent)
+        def _(copy=copy):
+            copy.wait_send()
+
+    @pl.when(relayed)
+    def _():
+        relay_in().wait_send()
+
+    @pl.when(last & (mine == 0))
+    def _():
+        relay_out(1, NEAR - 1).wait_send()
+        relay_out(2, NEAR - 2).wait_send()
+
+    @pl.when(last & (mine == 1))
+    def _():
+        relay_out(2, NEAR - 1).wait_send()
 
 
 def s_row_up(ref, g):
@@ -521,7 +578,6 @@
                 vmem(DOTS, LANES),
                 vmem(1, width),
                 vmem(blocks, width),
-                vmem(BAND + 1, blocks, width),
                 vmem(n, LANES),
                 dma((blocks * slots,)),
                 dma((blocks,)),
@@ -529,10 +585,10 @@
                 dma((4 * BAND,)),
                 dma((4 * BAND,)),
                 dma((BAND + 1,)),
-                dma((BAND + 1,)),
                 dma(()),
                 dma(()),
-                pltpu.SemaphoreType.REGULAR,
+                dma(()),
+                pltpu.SemaphoreType.REGULAR((2,)),
             ],
             compiler_params=pltpu.CompilerParams(
                 collective_id=0, has_side_effects=True, vmem_limit_bytes=60 << 20

time: 26.4 us -> 25.1 us (0.951)
  Pallas kernels: 25 us -> 23.8 us
    pallas_call x1, Pallas kernels: 25 us -> 23.8 us  [on_device(): pl.pallas_call(functools.partial(kernel, n), out_shape=[vmem(blocks, widt...]
where the time goes in v4:
time: 25.1 us; the launch traced here: 25 us
  Pallas kernels  23.8 us (95%)
  between operations  0.64 us (3%)
  other arithmetic  0.61 us (2%)
    pallas_call x1, Pallas kernels, on_device(): pl.pallas_call(functools.partial(kernel, n), out_shape=[vmem(blocks, widt...  23.8 us
    add x1, other arithmetic, on_device(): return (one * p - two * q, rhs - one * s + two * w)  0.61 us

profile of v4, /device:TPU:1, one launch (start us, length us, event | category | flops | bytes accessed | tf_op | source)
XLA Modules:
  0.0 25.0 jit_solution(1831644403438044947)
XLA Ops:
  0.6 23.8 %shard_map.68 = (f32[4,288]{1,0:T(4,128)S(1)}, f32[4,288]{1,0:T(4,128)S(1)}, f32[4,288]{1,0:T(4,128)S(1)}, f32[4,288]{1,0:T(4,128)S(1)}, f32[4,288]{1,0:T(4,128)...) custom-call(f32[4,288]{1,0:T(4,128)} %rhs_hbm.1, f32[4,4,288,288]{3,2,1,0:T(8,128)} %tiles_hbm.1, s32[4,4]{1,0:T(4,128)} %cols_hbm.1, ...), custom_call_target="tpu_custom_call" | custom-call | tf_op jit(solution)/shard_map/pallas_call | solution.py:556
  24.4 0.6 %multiply_add_fusion = (f32[4,288]{1,0:T(4,128)}, f32[4,288]{1,0:T(4,128)}) fusion(f32[4,288]{1,0:T(4,128)S(1)} %get-tuple-element.11, f32[4,288]{1,0:T(4,128)S(1)} %get-tuple-element.15, f32[4,288]{1,0:T(4,128)S(1)} %get-tuple-element.13, f32[4,288]{1,0:T(4,128)S(1)} %get-tuple-element.9, f32[4,288]{1,0:T(4,128)S(1)} %get-tuple-element.14, ...), kind=kLoop, calls=%fused_computation | loop fusion | flops 8064 | bytes 41472 | tf_op jit(solution)/shard_map/add | solution.py:597

commit v5 on v4

--- a/solution.py
+++ b/solution.py
@@ -73,10 +73,11 @@
         moved.append([lax.rem(place + step, size) * stride for step in range(size)])
     offsets = list(itertools.product(*[range(size) for size in sizes]))[1:]
 
-    def hops(offset):
-        return sum(min(o, s - o) for o, s in zip(offset[:-1], sizes[:-1])) + 0.1 * offset[-1]
-
-    for offset in sorted(offsets, key=hops):
+    def due(offset):
+        hops = sum(min(o, s - o) for o, s in zip(offset[:-1], sizes[:-1]))
+        return (offset[:3] != (2, 1, 0), offset[1:3] != (1, 0), offset[2] != 0, hops)
+
+    for offset in sorted(offsets, key=due):
         yield sum(axis[step] for axis, step in zip(moved[1:], offset[1:])) + moved[0][offset[0]]
 
 
@@ -113,6 +114,8 @@
     dots,
     cross,
     mid_p,
+    mid_q,
+    mid_low,
     everyone,
     tile_sem,
     minv_sem,
@@ -286,7 +289,7 @@
         )
 
     def relay_in():
-        return relay(0, p_ext.at[0], mid_p, mid_recv, ahead(-NEAR))
+        return relay(0, p_ext.at[0], mid_p, mid_recv.at[0], ahead(-NEAR))
 
     def relay_out(distance, place):
         return relay(
@@ -369,19 +372,16 @@
         relay_in().wait_recv()
         relay_out(2, NEAR - 1).start()
 
-    for copy in p_sends:
-        copy.wait_recv()
-    for g in range(blocks):
-        terms = [(tiles.at[g, k], picked(p_ext, g, k)) for k in range(1, slots)]
-        times_rows(terms, None, s_row.at[g : g + 1, :])
     for g in range(blocks):
         tile_copy[g, 0].wait()
         times_columns([tiles.at[g, 0]], p_col.at[g], [w_row.at[g : g + 1, :]])
     w_row[...] = w_row[...] + p_low[0]
+    for copy in p_sends:
+        copy.wait_recv()
+    for g in range(blocks):
+        terms = [(tiles.at[g, k], picked(p_ext, g, k)) for k in range(1, slots)]
+        times_rows(terms, None, s_row.at[g : g + 1, :])
     s_near = s_row[...] + w_row[...]
-    pl.semaphore_wait(ready.at[0], SIZES[n][1] - 1)
-    for d in range(1, NEAR):
-        pl.semaphore_signal(ready.at[1], inc=1, device_id=near_peer(d), device_id_type=MESH)
     for copy in low_sends:
         copy.wait_recv()
     s_row[...] = s_near + p_got[1] + p_got[2]
@@ -390,6 +390,25 @@
         times_rows(
             [(minv.at[g], s_row[g : g + 1, :])], q_col.at[g], q_ext.at[0, g : g + 1, :]
         )
+    def half_q():
+        return relay(BAND + 1, q_ext.at[0], mid_q, mid_recv.at[BAND + 1], ahead(-NEAR))
+
+    def half_low(distance, place):
+        return relay(
+            BAND + 1 + distance,
+            q_low.at[distance],
+            mid_low.at[distance],
+            mid_recv.at[distance],
+            (plane * NEAR + place,),
+        )
+
+    half_there = first & (plane != 0)
+    half_here = last & (plane != n // NEAR - 1)
+
+    @pl.when(half_there & (mine < BAND))
+    def _():
+        half_q().start()
+
     q_sends = [send(2 * BAND + d - 1, q_ext.at[0], q_ext.at[d], -d) for d in range(1, BAND + 1)]
     for copy in q_sends:
         copy.start()
@@ -397,10 +416,6 @@
     def put_dot(index, value):
         whole = jnp.sum(jnp.sum(value, axis=0, keepdims=True), axis=1, keepdims=True)
         dots[index : index + 1, :] = jnp.broadcast_to(whole, (1, LANES))
-
-    put_dot(0, rhs[...] * p_ext[0])
-    put_dot(1, p_ext[0] * s_row[...])
-    put_dot(2, s_row[...] * q_ext[0])
 
     for g in range(blocks):
         times_columns(
@@ -410,12 +425,28 @@
         )
     for d in range(1, BAND + 1):
         q_low[d] = spread(d)
+
+    @pl.when(half_here & (mine == NEAR - 1))
+    def _():
+        half_low(1, 0).start()
+        half_low(2, 1).start()
+
+    @pl.when(half_here & (mine == NEAR - 2))
+    def _():
+        half_low(2, 0).start()
 
     q_low_sends = [
         send(3 * BAND + d - 1, q_low.at[d], q_got.at[d], d) for d in range(1, BAND + 1)
     ]
     for copy in q_low_sends:
         copy.start()
+    pl.semaphore_wait(ready.at[0], SIZES[n][1] - 1)
+    for d in range(1, NEAR):
+        pl.semaphore_signal(ready.at[1], inc=1, device_id=near_peer(d), device_id_type=MESH)
+    put_dot(0, rhs[...] * p_ext[0])
+    put_dot(1, p_ext[0] * s_row[...])
+    put_dot(2, s_row[...] * q_ext[0])
+
     q_low[0] = spread(0)
     for g in range(blocks):
         times_columns([tiles.at[g, 0]], q_col.at[g], [w_row.at[g : g + 1, :]])
@@ -428,8 +459,9 @@
         cross[...] = cross[...] + 2.0 * jnp.sum(rows * low, axis=0, keepdims=True)
 
     here = [(mine < NEAR - 3) | (mine == NEAR - 2), mine < NEAR - 4]
-    both_there = (mine == 0) | (mine == NEAR - 2)
-    one_there = (mine == 1) | (mine == NEAR - 1)
+    edge = jnp.logical_not(half_there)
+    both_there = (edge & (mine == 0)) | (mine == NEAR - 2)
+    one_there = (edge & (mine == 1)) | (mine == NEAR - 1)
     got_there = [both_there, both_there | one_there]
     for copy, wanted, d in zip(q_sends, here, range(1, BAND + 1)):
 
@@ -444,6 +476,19 @@
         def _(copy=copy, d=d):
             copy.wait_recv()
             add_cross(q_ext[0], q_got[d])
+
+    @pl.when(half_here & (mine == 0))
+    def _():
+        half_q().wait_recv()
+        half_low(1, 0).wait_recv()
+        half_low(2, 0).wait_recv()
+        add_cross(mid_q[...], mid_low[1] + mid_low[2])
+
+    @pl.when(half_here & (mine == 1))
+    def _():
+        half_q().wait_recv()
+        half_low(2, 1).wait_recv()
+        add_cross(mid_q[...], mid_low[2])
 
     put_dot(3, cross[...])
     lane = lax.broadcasted_iota(jnp.int32, (1, LANES), 1)
@@ -535,6 +580,19 @@
     @pl.when(last & (mine == 1))
     def _():
         relay_out(2, NEAR - 1).wait_send()
+
+    @pl.when(half_there & (mine < BAND))
+    def _():
+        half_q().wait_send()
+
+    @pl.when(half_here & (mine == NEAR - 1))
+    def _():
+        half_low(1, 0).wait_send()
+        half_low(2, 1).wait_send()
+
+    @pl.when(half_here & (mine == NEAR - 2))
+    def _():
+        half_low(2, 0).wait_send()
 
 
 def s_row_up(ref, g):
@@ -578,14 +636,16 @@
                 vmem(DOTS, LANES),
                 vmem(1, width),
                 vmem(blocks, width),
+                vmem(blocks, width),
+                vmem(BAND + 1, blocks, width),
                 vmem(n, LANES),
                 dma((blocks * slots,)),
                 dma((blocks,)),
                 dma((3,)),
                 dma((4 * BAND,)),
                 dma((4 * BAND,)),
-                dma((BAND + 1,)),
-                dma(()),
+                dma((2 * BAND + 2,)),
+                dma((BAND + 2,)),
                 dma(()),
                 dma(()),
                 pltpu.SemaphoreType.REGULAR((2,)),

time: 25.1 us -> 24.4 us (0.972)
  Pallas kernels: 23.8 us -> 23 us
    pallas_call x1, Pallas kernels: 23.8 us -> 23 us  [on_device(): pl.pallas_call(functools.partial(kernel, n), out_shape=[vmem(blocks, widt...]
where the time goes in v5:
time: 24.4 us; the launch traced here: 24.2 us
  Pallas kernels  23 us (94%)
  between operations  0.64 us (3%)
  other arithmetic  0.61 us (2%)
    pallas_call x1, Pallas kernels, on_device(): pl.pallas_call(functools.partial(kernel, n), out_shape=[vmem(blocks, widt...  23 us
    add x1, other arithmetic, on_device(): return (one * p - two * q, rhs - one * s + two * w)  0.61 us

profile of v5, /device:TPU:1, one launch (start us, length us, event | category | flops | bytes accessed | tf_op | source)
XLA Modules:
  0.0 24.2 jit_solution(542404699530535932)
XLA Ops:
  0.6 23.0 %shard_map.68 = (f32[4,288]{1,0:T(4,128)S(1)}, f32[4,288]{1,0:T(4,128)S(1)}, f32[4,288]{1,0:T(4,128)S(1)}, f32[4,288]{1,0:T(4,128)S(1)}, f32[4,288]{1,0:T(4,128)...) custom-call(f32[4,288]{1,0:T(4,128)} %rhs_hbm.1, f32[4,4,288,288]{3,2,1,0:T(8,128)} %tiles_hbm.1, s32[4,4]{1,0:T(4,128)} %cols_hbm.1, ...), custom_call_target="tpu_custom_call" | custom-call | tf_op jit(solution)/shard_map/pallas_call | solution.py:614
  23.6 0.6 %multiply_add_fusion = (f32[4,288]{1,0:T(4,128)}, f32[4,288]{1,0:T(4,128)}) fusion(f32[4,288]{1,0:T(4,128)S(1)} %get-tuple-element.11, f32[4,288]{1,0:T(4,128)S(1)} %get-tuple-element.15, f32[4,288]{1,0:T(4,128)S(1)} %get-tuple-element.13, f32[4,288]{1,0:T(4,128)S(1)} %get-tuple-element.9, f32[4,288]{1,0:T(4,128)S(1)} %get-tuple-element.14, ...), kind=kLoop, calls=%fused_computation | loop fusion | flops 8064 | bytes 41472 | tf_op jit(solution)/shard_map/add | solution.py:657

commit v6 on v5

--- a/solution.py
+++ b/solution.py
@@ -23,8 +23,10 @@
 
 
 def fold_rows(value):
-    rows, width = value.shape
-    return jnp.sum(value.reshape(rows // 8, 8, width), axis=0)
+    total = value[0:8, :]
+    for at in range(8, value.shape[0], 8):
+        total = total + value[at : at + 8, :]
+    return total
 
 
 def two_sum(a, b):
@@ -107,8 +109,7 @@
     s_row,
     w_row,
     prods,
-    p_low,
-    q_low,
+    lows,
     p_got,
     q_got,
     dots,
@@ -129,6 +130,7 @@
     ready,
 ):
     blocks, slots, width, _ = tiles.shape
+    p_low, q_low = lows.at[pl.ds(0, BAND + 1)], lows.at[pl.ds(BAND + 1, BAND + 1)]
     far = n // NEAR
     me = lax.axis_index(AXIS)
     mine = lax.rem(me, NEAR)
@@ -144,21 +146,21 @@
     minv_copy = [
         pltpu.make_async_copy(minv_hbm.at[g], minv.at[g], minv_sem.at[g]) for g in range(blocks)
     ]
-    tile_copy = {
-        (g, k): pltpu.make_async_copy(
-            tiles_hbm.at[g, k], tiles.at[g, k], tile_sem.at[g * slots + k]
+    tile_copy = [
+        pltpu.make_async_copy(
+            tiles_hbm.at[g, pl.ds(1, slots - 1)], tiles.at[g, pl.ds(1, slots - 1)], tile_sem.at[g]
         )
         for g in range(blocks)
-        for k in range(slots)
-    }
-    def start_tiles(g):
-        for k in range(1, slots):
-            tile_copy[g, k].start()
+    ]
+    diag_copy = [
+        pltpu.make_async_copy(tiles_hbm.at[g, 0], tiles.at[g, 0], tile_sem.at[blocks])
+        for g in range(blocks)
+    ]
 
     small[0].start()
     for copy in minv_copy:
         copy.start()
-    start_tiles(0)
+    tile_copy[0].start()
 
     def ahead(steps):
         return (lax.rem(me + n + steps, n),)
@@ -218,7 +220,7 @@
         return pltpu.make_async_remote_copy(
             src_ref=source,
             dst_ref=target,
-            send_sem=halo_send.at[index],
+            send_sem=halo_send.at[min(index, BAND)],
             recv_sem=halo_recv.at[index],
             device_id=ahead(steps),
             device_id_type=MESH,
@@ -263,14 +265,14 @@
             for (low, high), value in zip(groups, sums[index]):
                 row_out[:, low:high] = jnp.sum(value, axis=0, keepdims=True)
 
-    start_tiles(1)
+    tile_copy[1].start()
     small[1].start()
     small[2].start()
     small[0].wait()
     for g in range(blocks):
         minv_copy[g].wait()
         if g + 2 < blocks:
-            start_tiles(g + 2)
+            tile_copy[g + 2].start()
         times_rows(
             [(minv.at[g], rhs[g : g + 1, :])], p_col.at[g], p_ext.at[0, g : g + 1, :]
         )
@@ -346,9 +348,8 @@
         return prods.at[slot : slot + 1, :]
 
     for g in range(blocks):
-        for k in range(1, slots):
-            tile_copy[g, k].wait()
-        tile_copy[g, 0].start()
+        tile_copy[g].wait()
+        diag_copy[g].start()
         times_columns(
             [tiles.at[g, k] for k in range(1, slots)],
             p_col.at[g],
@@ -372,8 +373,9 @@
         relay_in().wait_recv()
         relay_out(2, NEAR - 1).start()
 
-    for g in range(blocks):
-        tile_copy[g, 0].wait()
+    diagonals = tiles.at[pl.ds(0, blocks), 0]
+    pltpu.make_async_copy(diagonals, diagonals, tile_sem.at[blocks]).wait()
+    for g in range(blocks):
         times_columns([tiles.at[g, 0]], p_col.at[g], [w_row.at[g : g + 1, :]])
     w_row[...] = w_row[...] + p_low[0]
     for copy in p_sends:
@@ -391,11 +393,11 @@
             [(minv.at[g], s_row[g : g + 1, :])], q_col.at[g], q_ext.at[0, g : g + 1, :]
         )
     def half_q():
-        return relay(BAND + 1, q_ext.at[0], mid_q, mid_recv.at[BAND + 1], ahead(-NEAR))
+        return relay(0, q_ext.at[0], mid_q, mid_recv.at[BAND + 1], ahead(-NEAR))
 
     def half_low(distance, place):
         return relay(
-            BAND + 1 + distance,
+            distance,
             q_low.at[distance],
             mid_low.at[distance],
             mid_recv.at[distance],
@@ -404,6 +406,10 @@
 
     half_there = first & (plane != 0)
     half_here = last & (plane != n // NEAR - 1)
+
+    @pl.when(relayed)
+    def _():
+        relay_in().wait_send()
 
     @pl.when(half_there & (mine < BAND))
     def _():
@@ -558,8 +564,8 @@
     two_out[...] = jnp.broadcast_to(two, (blocks, width))
     w_out[...] = w_row[...]
 
-    for copy in low_sends + q_sends + q_low_sends:
-        copy.wait_send()
+    assert len(low_sends + q_sends + q_low_sends) == lows.shape[0]
+    pltpu.make_async_copy(lows, lows, halo_send.at[BAND]).wait()
     pltpu.make_async_copy(others, others, all_send).wait()
 
     for copy, sent in zip(p_sends, direct):
@@ -567,10 +573,6 @@
         @pl.when(sent)
         def _(copy=copy):
             copy.wait_send()
-
-    @pl.when(relayed)
-    def _():
-        relay_in().wait_send()
 
     @pl.when(last & (mine == 0))
     def _():
@@ -629,8 +631,7 @@
                 vmem(blocks, width),
                 vmem(blocks, width),
                 vmem(blocks * slots, width),
-                vmem(BAND + 1, blocks, width),
-                vmem(BAND + 1, blocks, width),
+                vmem(2 * BAND + 2, blocks, width),
                 vmem(BAND + 1, blocks, width),
                 vmem(BAND + 1, blocks, width),
                 vmem(DOTS, LANES),
@@ -639,12 +640,12 @@
                 vmem(blocks, width),
                 vmem(BAND + 1, blocks, width),
                 vmem(n, LANES),
-                dma((blocks * slots,)),
+                dma((blocks + 1,)),
                 dma((blocks,)),
                 dma((3,)),
+                dma((BAND + 1,)),
                 dma((4 * BAND,)),
-                dma((4 * BAND,)),
-                dma((2 * BAND + 2,)),
+                dma((BAND + 1,)),
                 dma((BAND + 2,)),
                 dma(()),
                 dma(()),

time: 24.4 us -> 24.2 us (level)
  no operation moved by 1% of the time
where the time goes in v6:
time: 24.2 us; the launch traced here: 24.1 us
  Pallas kernels  22.9 us (95%)
  between operations  0.64 us (3%)
  other arithmetic  0.61 us (3%)
    pallas_call x1, Pallas kernels, on_device(): pl.pallas_call(functools.partial(kernel, n), out_shape=[vmem(blocks, widt...  22.9 us
    add x1, other arithmetic, on_device(): return (one * p - two * q, rhs - one * s + two * w)  0.61 us

profile of v6, /device:TPU:1, one launch (start us, length us, event | category | flops | bytes accessed | tf_op | source)
XLA Modules:
  0.0 24.1 jit_solution(14107488793031498515)
XLA Ops:
  0.6 22.9 %shard_map.68 = (f32[4,288]{1,0:T(4,128)S(1)}, f32[4,288]{1,0:T(4,128)S(1)}, f32[4,288]{1,0:T(4,128)S(1)}, f32[4,288]{1,0:T(4,128)S(1)}, f32[4,288]{1,0:T(4,128)...) custom-call(f32[4,288]{1,0:T(4,128)} %rhs_hbm.1, f32[4,4,288,288]{3,2,1,0:T(8,128)} %tiles_hbm.1, s32[4,4]{1,0:T(4,128)} %cols_hbm.1, ...), custom_call_target="tpu_custom_call" | custom-call | tf_op jit(solution)/shard_map/pallas_call | solution.py:616
  23.5 0.6 %multiply_add_fusion = (f32[4,288]{1,0:T(4,128)}, f32[4,288]{1,0:T(4,128)}) fusion(f32[4,288]{1,0:T(4,128)S(1)} %get-tuple-element.11, f32[4,288]{1,0:T(4,128)S(1)} %get-tuple-element.15, f32[4,288]{1,0:T(4,128)S(1)} %get-tuple-element.13, f32[4,288]{1,0:T(4,128)S(1)} %get-tuple-element.9, f32[4,288]{1,0:T(4,128)S(1)} %get-tuple-element.14, ...), kind=kLoop, calls=%fused_computation | loop fusion | flops 8064 | bytes 41472 | tf_op jit(solution)/shard_map/add | solution.py:658

commit v7 on v6

--- a/solution.py
+++ b/solution.py
@@ -14,7 +14,7 @@
 NEAR = 8
 BAND = 2
 DOTS = 4
-SIZES = {128: (4, 4, 4, 2), 16: (1, 2, 4, 2)}
+SIZES = {128: (4, 4, 4, 2), 32: (2, 2, 4, 2)}
 AXIS = "cams"
 
 
@@ -77,7 +77,7 @@
 
     def due(offset):
         hops = sum(min(o, s - o) for o, s in zip(offset[:-1], sizes[:-1]))
-        return (offset[:3] != (2, 1, 0), offset[1:3] != (1, 0), offset[2] != 0, hops)
+        return (offset[:3] != (1, 1, 0), offset[1:3] != (1, 0), offset[2] != 0, hops)
 
     for offset in sorted(offsets, key=due):
         yield sum(axis[step] for axis, step in zip(moved[1:], offset[1:])) + moved[0][offset[0]]
@@ -179,9 +179,10 @@
             moved = plane + (lax.rem(place + step, size) - place) * stride
             yield (moved * NEAR + mine,)
 
-    line = lax.rem(plane, SIZES[n][1])
+    lines = SIZES[n][1]
+    line = lax.rem(plane, lines)
     first = line == 0
-    last = line == SIZES[n][1] - 1
+    last = line == lines - 1
     relayed = first & (mine < BAND)
 
     barrier = pltpu.get_barrier_semaphore()
@@ -393,7 +394,8 @@
             [(minv.at[g], s_row[g : g + 1, :])], q_col.at[g], q_ext.at[0, g : g + 1, :]
         )
     def half_q():
-        return relay(0, q_ext.at[0], mid_q, mid_recv.at[BAND + 1], ahead(-NEAR))
+        peer = (jnp.where(outer_there, plane + lines - 1, plane - 1) * NEAR + mine,)
+        return relay(0, q_ext.at[0], mid_q, mid_recv.at[BAND + 1], peer)
 
     def half_low(distance, place):
         return relay(
@@ -401,11 +403,14 @@
             q_low.at[distance],
             mid_low.at[distance],
             mid_recv.at[distance],
-            (plane * NEAR + place,),
+            (jnp.where(outer_from, plane + lines, plane) * NEAR + place,),
         )
 
     half_there = first & (plane != 0)
-    half_here = last & (plane != n // NEAR - 1)
+    half_from = last & (plane != n // NEAR - 1)
+    outer_from = plane == n // NEAR - lines - 1
+    outer_there = plane == n // NEAR - lines
+    half_here = last & jnp.logical_not(outer_from)
 
     @pl.when(relayed)
     def _():
@@ -432,12 +437,12 @@
     for d in range(1, BAND + 1):
         q_low[d] = spread(d)
 
-    @pl.when(half_here & (mine == NEAR - 1))
+    @pl.when(half_from & (mine == NEAR - 1))
     def _():
         half_low(1, 0).start()
         half_low(2, 1).start()
 
-    @pl.when(half_here & (mine == NEAR - 2))
+    @pl.when(half_from & (mine == NEAR - 2))
     def _():
         half_low(2, 0).start()
 
@@ -587,12 +592,12 @@
     def _():
         half_q().wait_send()
 
-    @pl.when(half_here & (mine == NEAR - 1))
+    @pl.when(half_from & (mine == NEAR - 1))
     def _():
         half_low(1, 0).wait_send()
         half_low(2, 1).wait_send()
 
-    @pl.when(half_here & (mine == NEAR - 2))
+    @pl.when(half_from & (mine == NEAR - 2))
     def _():
         half_low(2, 0).wait_send()
 

time: 24.2 us -> 24.1 us (level)
  no operation moved by 1% of the time
where the time goes in v7:
time: 24.1 us; the launch traced here: 24 us
  Pallas kernels  22.7 us (94%)
  between operations  0.64 us (3%)
  other arithmetic  0.61 us (3%)
    pallas_call x1, Pallas kernels, on_device(): pl.pallas_call(functools.partial(kernel, n), out_shape=[vmem(blocks, widt...  22.7 us
    add x1, other arithmetic, on_device(): return (one * p - two * q, rhs - one * s + two * w)  0.61 us

profile of v7, /device:TPU:1, one launch (start us, length us, event | category | flops | bytes accessed | tf_op | source)
XLA Modules:
  0.0 24.0 jit_solution(11401589319925236241)
XLA Ops:
  0.6 22.7 %shard_map.68 = (f32[4,288]{1,0:T(4,128)S(1)}, f32[4,288]{1,0:T(4,128)S(1)}, f32[4,288]{1,0:T(4,128)S(1)}, f32[4,288]{1,0:T(4,128)S(1)}, f32[4,288]{1,0:T(4,128)...) custom-call(f32[4,288]{1,0:T(4,128)} %rhs_hbm.1, f32[4,4,288,288]{3,2,1,0:T(8,128)} %tiles_hbm.1, s32[4,4]{1,0:T(4,128)} %cols_hbm.1, ...), custom_call_target="tpu_custom_call" | custom-call | tf_op jit(solution)/shard_map/pallas_call | solution.py:621
  23.4 0.6 %multiply_add_fusion = (f32[4,288]{1,0:T(4,128)}, f32[4,288]{1,0:T(4,128)}) fusion(f32[4,288]{1,0:T(4,128)S(1)} %get-tuple-element.11, f32[4,288]{1,0:T(4,128)S(1)} %get-tuple-element.15, f32[4,288]{1,0:T(4,128)S(1)} %get-tuple-element.13, f32[4,288]{1,0:T(4,128)S(1)} %get-tuple-element.9, f32[4,288]{1,0:T(4,128)S(1)} %get-tuple-element.14, ...), kind=kLoop, calls=%fused_computation | loop fusion | flops 8064 | bytes 41472 | tf_op jit(solution)/shard_map/add | solution.py:663
